TPU v7x, 512 devices: a whole 4x4x16 slice. The times are simulated.
512 devices in a mesh: step: 16 (over z), band: 32 (over x, y, core).
Axes of the slice: x: 4, y: 4, z: 16, core: 2. Of those that a mesh axis runs over, the one named last changes fastest.
Arguments:
- states: float32 [16, 64, 10752], P('step', 'band'), may hold values from -6 to 6
- anchor: float32 [64, 10752], P('band'), may hold values from -6 to 6
- step_index: int32 [16], P('step'), may hold values from 0 to 19
- sigmas: float32 [20], replicated, may hold values from 0.05 to 0.5
- enc_w: bfloat16 [84, 512], replicated, may hold values from -0.625 to 0.625
- noise_embed: float32 [512], replicated, may hold values from -3 to 3
- qkv_w: bfloat16 [512, 1536], replicated, may hold values from -0.25 to 0.25
- out_w: bfloat16 [512, 512], replicated, may hold values from -0.25 to 0.25
- up_w: bfloat16 [512, 1024], replicated, may hold values from -0.25 to 0.25
- down_w: bfloat16 [1024, 512], replicated, may hold values from -0.1875 to 0.1875
- dec_w: bfloat16 [512, 84], replicated, may hold values from -0.25 to 0.25
Outputs:
- new_states: float32 [16, 64, 10752], P('step', 'band')
- change: float32 [16], P('step')
All inputs are finite; a program needn't handle non-finite values.
Results may differ from a plain program's by a relative error of at most 0.0031.
Values may be sent and summed in bfloat16 or wider, within the bound.
No kernel may reach another device: no remote copies, remote signals or barrier semaphores. Data moves between devices by JAX's collectives and lax.ppermute only.
A program may use at most 64 MiB of HBM per device.

v0:
```python
import math

import jax
import jax.numpy as jnp
from jax import lax
from jax.sharding import PartitionSpec as P

C = 84
W = 512
HEADS = 4
HEAD_DIM = 128
LEVELS = 20
R = 2


epsilon = 1e-06
score_gain = 3.0


def passed_along(array, axis, by):
    length = lax.axis_size(axis)
    pairs = [(i, i + by) for i in range(length) if 0 <= i + by < length]
    return lax.ppermute(array, axis, pairs)


def with_halo(array, sides, width):
    for axis, dim in sides:
        size, length = (lax.axis_size(axis), array.shape[dim])
        up = [(i, (i + 1) % size) for i in range(size - 1)]
        down = [(j, i) for i, j in up]
        last = lax.slice_in_dim(array, length - width, length, axis=dim)
        initial = lax.slice_in_dim(array, 0, width, axis=dim)
        before = lax.ppermute(last, axis, up)
        after = lax.ppermute(initial, axis, down)
        array = jnp.concatenate([before, array, after], axis=dim)
    return array


def carried_in(part, axis, combine, identity):
    place = lax.axis_index(axis)
    gathered = lax.all_gather(part, axis)
    state = jnp.zeros_like(part) + jnp.asarray(identity, part.dtype)

    def one(turn, state):
        return combine(state, lax.dynamic_index_in_dim(gathered, turn, 0, False))

    return lax.fori_loop(0, place, one, state)


def rms_scale(values):
    return values * lax.rsqrt(jnp.mean(values * values, axis=-1, keepdims=True) + epsilon)


def split_heads(projected):
    heads = rms_scale(projected.reshape(projected.shape[0], HEADS, HEAD_DIM))
    return heads.astype(jnp.bfloat16)


def embed_rows(fields, enc_w, offset_vec):
    tokens = fields.reshape(-1, C)
    embedded = jnp.dot(tokens, enc_w, preferred_element_type=jnp.float32) + offset_vec[None, :]
    return (embedded, rms_scale(embedded).astype(jnp.bfloat16))


def window_mask_for(first_row, lat_rows, total_rows):
    offsets = jnp.arange(lat_rows + 2 * R, dtype=jnp.int32) - R
    key_rows = first_row + offsets
    inside = (key_rows >= 0) & (key_rows < total_rows)
    near = jnp.abs(jnp.arange(lat_rows, dtype=jnp.int32)[:, None] - offsets[None, :]) <= R
    return (inside[None, :] & near).astype(jnp.float32)


def attend(queries, key_heads, value_heads, window_mask):
    scores = jnp.einsum("qhd,khd->hqk", queries, key_heads, preferred_element_type=jnp.float32)
    scores = scores * (score_gain / math.sqrt(HEAD_DIM))
    heads, count_q, count_k = scores.shape
    rows_q = window_mask.shape[0]
    rows_k = window_mask.shape[1]
    columns = count_q // rows_q
    weights = jnp.exp(scores).reshape(heads, rows_q, columns, rows_k, columns)
    weights = (weights * window_mask[None, :, None, :, None]).reshape(heads, count_q, count_k)
    softmax_weights = (weights / jnp.sum(weights, axis=-1, keepdims=True)).astype(jnp.bfloat16)
    attended = jnp.einsum(
        "hqk,khd->qhd", softmax_weights, value_heads, preferred_element_type=jnp.float32
    )
    return attended.astype(jnp.bfloat16).reshape(count_q, W)


def finish_block(embedded, attended, out_w, up_w, down_w, dec_w):
    mixed = embedded + jnp.dot(attended, out_w, preferred_element_type=jnp.float32)
    normed = rms_scale(mixed).astype(jnp.bfloat16)
    hidden = jax.nn.gelu(jnp.dot(normed, up_w, preferred_element_type=jnp.float32)).astype(
        jnp.bfloat16
    )
    mixed = mixed + jnp.dot(hidden, down_w, preferred_element_type=jnp.float32)
    return jnp.dot(rms_scale(mixed).astype(jnp.bfloat16), dec_w, preferred_element_type=jnp.float32)


def add_fields(earlier, later):
    return earlier + later


def local(
    states, anchor, step_index, sigmas, enc_w, noise_embed, qkv_w, out_w, up_w, down_w, dec_w
):
    steps_here, lat_rows, field_width = states.shape
    columns = field_width // C
    total_rows = lat_rows * lax.axis_size("band")
    first_row = lax.axis_index("band") * lat_rows
    previous = passed_along(states.astype(jnp.bfloat16), "step", 1).astype(states.dtype)
    opening = jnp.where(lax.axis_index("step") == 0, anchor[None], previous)
    inputs = jnp.concatenate([opening, states[:-1]], axis=0)
    onehot = (step_index[:, None] == jnp.arange(LEVELS, dtype=jnp.int32)[None, :]).astype(
        jnp.float32
    )
    noise_levels = jnp.sum(onehot * sigmas[None, :], axis=1)
    fields = inputs.astype(jnp.bfloat16)
    window_mask = window_mask_for(first_row, lat_rows, total_rows)
    local_step = 0
    offset_vec = jnp.log(noise_levels[local_step]) * noise_embed
    embedded, normed = embed_rows(fields[local_step], enc_w, offset_vec)
    projected = jnp.dot(normed, qkv_w, preferred_element_type=jnp.float32)
    query_list = [split_heads(projected[:, :W])]
    embed_list = [embedded]
    key_grid = split_heads(projected[:, W : 2 * W]).reshape(lat_rows, columns, W)
    value_grid = projected[:, 2 * W :].astype(jnp.bfloat16).reshape(lat_rows, columns, W)
    stacked_list = [jnp.stack([key_grid, value_grid], axis=0)]
    stacked = jnp.stack(stacked_list, axis=0)
    widened = with_halo(stacked, (("band", 2),), R)
    local_step = 0
    key_heads = widened[local_step, 0].reshape(-1, HEADS, HEAD_DIM)
    value_heads = widened[local_step, 1].reshape(-1, HEADS, HEAD_DIM)
    attended = attend(query_list[local_step], key_heads, value_heads, window_mask)
    drift_list = [finish_block(embed_list[local_step], attended, out_w, up_w, down_w, dec_w)]
    drifts = jnp.stack(
        [drift_rows.reshape(lat_rows, field_width) for drift_rows in drift_list], axis=0
    )
    running = jnp.cumsum(noise_levels[:, None, None] * drifts, axis=0)
    block_total = running[-1]
    earlier = carried_in(block_total, "step", add_fields, jnp.zeros_like(block_total))
    new_states = anchor[None] + (earlier[None] + running)
    latitude = (
        jnp.pi
        * ((first_row + jnp.arange(lat_rows, dtype=jnp.int32)).astype(jnp.float32) + 0.5)
        / total_rows
        - 0.5 * jnp.pi
    )
    area = jnp.cos(latitude)
    all_latitude = jnp.pi * ((jnp.arange(total_rows, dtype=jnp.float32) + 0.5) / total_rows - 0.5)
    area_total = jnp.sum(jnp.cos(all_latitude))
    mismatch = new_states - states
    partial_value = jnp.sum(area[None, :, None] * mismatch * mismatch, axis=(1, 2))
    change = lax.psum(partial_value, "band") / (area_total * field_width)
    return (new_states, change)


def solution(mesh):
    placed = (
        P("step", "band", None),
        P("band", None),
        P("step"),
        P(),
        P(),
        P(),
        P(),
        P(),
        P(),
        P(),
        P(),
    )
    return jax.shard_map(
        local,
        mesh=mesh,
        in_specs=placed,
        out_specs=(P("step", "band", None), P("step")),
        check_vma=False,
    )
```

profile of v0, /device:TPU:481, one launch (start us, length us, event | category | flops | bytes accessed | tf_op | source)
XLA Modules:
  0.0 213.7 jit_solution(6867258895659570562)
XLA Ops:
  7.2 1.0 convert_element_type.59
  8.3 1.3 collective-permute-start
  10.2 1.3 fusion.28
  12.2 0.7 broadcast_multiply_fusion
  13.4 1.1 copy.36
  15.1 0.6 fusion.19
  15.7 1.0 fusion.35
  16.8 2.0 mul.171
  18.8 1.4 reduce_sum.85
  20.3 1.1 mul.172
  21.4 2.1 mul.173
  23.5 1.1 multiply_convert_fusion.3
  24.6 0.8 maximum_bitcast_fusion
  25.4 3.8 %collective-permute-start.1 = (bf16[1,2,2,128,512]{4,3,2,1,0:T(8,128)(2,1)}, bf16[1,2,2,128,512]{4,3,2,1,0:T(8,128)(2,1)}, u32[]{:S(2)}, u32[]{:S(2)}) collective-permute-start(bf16[1,2,2,128,512]{4,3,2,1,0:T(8,128)(2,1)} %maximum_bitcast_fusion), channel_id=1, source_target_pairs={{0,1},{1,2},{2,3},{3,4},{4,5},{5,6},{6,7},{7,8},{8,9},{9,10},{10,1... | collective-permute-start | bytes 1572872 | tf_op jit(solution)/shard_map/ppermute | solution.py:33
  29.2 1.9 collective-permute-start.2
  31.3 0.3 multiply_reduce_fusion.2
  32.0 3.6 %collective-permute-done.1 = bf16[1,2,2,128,512]{4,3,2,1,0:T(8,128)(2,1)} collective-permute-done((bf16[1,2,2,128,512]{4,3,2,1,0:T(8,128)(2,1)}, bf16[1,2,2,128,512]{4,3,2,1,0:T(8,128)(2,1)}, u32[]{:S(2)}, u32[]{:S(2)}) %collective-permute-start.1) | collective-permute-done | bytes 524320 | tf_op jit(solution)/shard_map/ppermute | solution.py:33
  35.6 4.4 %collective-permute-done.2 = bf16[1,2,2,128,512]{4,3,2,1,0:T(8,128)(2,1)} collective-permute-done((bf16[1,2,2,128,512]{4,3,2,1,0:T(8,128)(2,1)}, bf16[1,2,2,128,512]{4,3,2,1,0:T(8,128)(2,1)}, u32[]{:S(2)}, u32[]{:S(2)}) %collective-permute-start.2) | collective-permute-done | bytes 524320 | tf_op jit(solution)/shard_map/ppermute | solution.py:34
  40.0 1.5 pad_maximum_fusion
  41.5 1.0 fusion.34
  42.6 2.5 %reshape_squeeze.11 = bf16[768,4,128]{2,1,0:T(4,128)(2,1)} reshape(bf16[1,1,6,128,512]{4,3,2,1,0:T(8,128)(2,1)} %get-tuple-element.37) | data formatting | bytes 1572864 | tf_op jit(solution)/shard_map/reshape;squeeze | solution.py:131
  45.0 1.1 reshape_squeeze.10
  46.1 2.5 %fusion = (f32[4,256]{1,0:T(4,128)S(1)}, f32[4,256,768]{2,1,0:T(8,128)S(1)}) fusion(f32[256,768]{1,0:T(8,128)} %copy.36, bf16[768,4,128]{2,1,0:T(4,128)(2,1)} %reshape_squeeze.11, bf16[256,4,128]{2,1,0:T(4,128)(2,1)S(1)} %multiply_convert_fusion.2), kind=kOutput, calls=%fused_computation.3 | convolution fusion | flops 203684864 | bytes 4984832 | tf_op jit(solution)/shard_map/qhd,khd->hqk/dot_general | solution.py:74
  48.6 0.9 fusion.2
  49.6 0.4 multiply_reduce_fusion.1
  50.1 2.6 %multiply_reduce_fusion = (f32[256]{0:T(256)S(1)}, f32[256,512]{1,0:T(8,128)S(1)}) fusion(f32[256,512]{1,0:T(8,128)S(1)} %get-tuple-element.46, bf16[1024,512]{1,0:T(8,128)(2,1)} %param.22, bf16[512,1024]{1,0:T(8,128)(2,1)} %param.21, f32[256]{0:T(256)S(1)} %add_rsqrt_fusion.3), kind=kOutput, calls=%fused_computation.27 | convolution fusion | flops 539885312 | bytes 3147776 | tf_op jit(solution)/shard_map/dot_general | solution.py:95
  52.7 1.0 convolution_multiply_fusion
  53.8 0.8 mul.199
  54.6 0.7 cosine_reduce_fusion
  56.1 59.5 %all-gather.2.cloned.1.call-done = f32[16,2,10752]{2,1,0:T(2,128)} async-done(((f32[1,2,10752]{2,1,0:T(2,128)}), f32[16,2,10752]{2,1,0:T(2,128)}) %all-gather.2.cloned.1.call-update) | async-done | bytes 1376272 | tf_op jit(solution)/shard_map/all_gather | solution.py:41
  115.7 14.6 %while.10 = (s32[]{:T(128)}, f32[2,10752]{1,0:T(2,128)S(1)}, s32[]{:T(128)}, f32[16,2,10752]{2,1,0:T(2,128)}, s32[]{:T(128)}, /*index=5*/s32[]{:T(128)}, s32[]{:T(128)}) while((s32[]{:T(128)}, f32[2,10752]{1,0:T(2,128)S(1)}, s32[]{:T(128)}, f32[16,2,10752]{2,1,0:T(2,128)}, s32[]{:T(128)}, /*index=5*/s32[]{:T(128)}, s32[]{:T(128)}) %tuple.30), condition=%wide.region_8.9_spmd, body=%wide.region_7.8_spmd.sunk | while | flops 21509 | bytes 258163 | solution.py:47
  115.7 0.9 bitcast_add_fusion.2
  116.7 0.9 bitcast_add_fusion.2
  117.7 0.9 bitcast_add_fusion.2
  118.6 0.9 bitcast_add_fusion.2
  119.6 0.9 bitcast_add_fusion.2
  120.6 0.9 bitcast_add_fusion.2
  121.5 0.9 bitcast_add_fusion.2
  122.5 0.9 bitcast_add_fusion.2
  123.5 0.9 bitcast_add_fusion.2
  124.4 0.9 bitcast_add_fusion.2
  125.4 0.9 bitcast_add_fusion.2
  126.4 0.9 bitcast_add_fusion.2
  127.4 0.9 bitcast_add_fusion.2
  128.3 0.9 bitcast_add_fusion.2
  129.3 0.9 bitcast_add_fusion.2
  130.3 1.3 fusion.26
  131.6 73.5 %psum.7 = f32[1]{0:T(128)} all-reduce(f32[1]{0:T(128)} %bitcast.9), channel_id=1, replica_groups=mesh['step'=16,'band'=32] {'band'}, use_global_device_ids=true, to_apply=%region_10.11 | all-reduce | flops 1 | bytes 8 | tf_op jit(solution)/shard_map/psum | solution.py:153
  (42 shorter events, 2.2 us)
Async XLA Ops:
  7.2 8.0 %copy-start = (bf16[512,1536]{1,0:T(8,128)(2,1)S(1)}, bf16[512,1536]{1,0:T(8,128)(2,1)}, u32[]{:S(2)}) copy-start(bf16[512,1536]{1,0:T(8,128)(2,1)} %param.19) | copy-start | bytes 4718596
  7.2 108.5 %all-gather.2.cloned.1.call-start = ((), (), s32[]{:S(2)}) async-start(), calls=%async_computation | async-start | bytes 1462272 | tf_op jit(solution)/shard_map/all_gather | solution.py:41
  8.3 6.2 %collective-permute-start = (bf16[1,2,10752]{2,1,0:T(2,128)(2,1)S(1)}, bf16[1,2,10752]{2,1,0:T(2,128)(2,1)S(1)}, u32[]{:S(2)}, u32[]{:S(2)}) collective-permute-start(bf16[1,2,10752]{2,1,0:T(2,128)(2,1)S(1)} %convert_element_type.59), channel_id=1, source_target_pairs={{0,32},{32,64},{64,96},{96,128},{128,160},{160,192},{192,224},{224... | collective-permute-start | bytes 129032 | tf_op jit(solution)/shard_map/ppermute | solution.py:23
  13.3 1.2 copy-start.5
  13.3 1.5 copy-start.8
  25.4 10.2 %collective-permute-start.1 = (bf16[1,2,2,128,512]{4,3,2,1,0:T(8,128)(2,1)}, bf16[1,2,2,128,512]{4,3,2,1,0:T(8,128)(2,1)}, u32[]{:S(2)}, u32[]{:S(2)}) collective-permute-start(bf16[1,2,2,128,512]{4,3,2,1,0:T(8,128)(2,1)} %maximum_bitcast_fusion), channel_id=1, source_target_pairs={{0,1},{1,2},{2,3},{3,4},{4,5},{5,6},{6,7},{7,8},{8,9},{9,10},{10,1... | collective-permute-start | bytes 1572872 | tf_op jit(solution)/shard_map/ppermute | solution.py:33
  29.2 10.8 %collective-permute-start.2 = (bf16[1,2,2,128,512]{4,3,2,1,0:T(8,128)(2,1)}, bf16[1,2,2,128,512]{4,3,2,1,0:T(8,128)(2,1)}, u32[]{:S(2)}, u32[]{:S(2)}) collective-permute-start(bf16[1,2,2,128,512]{4,3,2,1,0:T(8,128)(2,1)} %maximum_bitcast_fusion), channel_id=1, source_target_pairs={{1,0},{2,1},{3,2},{4,3},{5,4},{6,5},{7,6},{8,7},{9,8},{10,9},{11,1... | collective-permute-start | bytes 1572872 | tf_op jit(solution)/shard_map/ppermute | solution.py:34
  46.1 2.5 %copy-start.1 = (f32[256,768]{1,0:T(8,128)S(1)}, f32[256,768]{1,0:T(8,128)}, u32[]{:S(2)}) copy-start(f32[256,768]{1,0:T(8,128)} %copy.36) | copy-start | bytes 2359300
  46.1 2.5 %copy-start.2 = (bf16[768,4,128]{2,1,0:T(4,128)(2,1)S(1)}, bf16[768,4,128]{2,1,0:T(4,128)(2,1)}, u32[]{:S(2)}) copy-start(bf16[768,4,128]{2,1,0:T(4,128)(2,1)} %reshape_squeeze.10) | copy-start | bytes 2359300
  48.6 1.0 copy-start.3
  50.1 2.6 %copy-start.7 = (bf16[512,84]{0,1:T(8,128)(2,1)S(1)}, bf16[512,84]{0,1:T(8,128)(2,1)}, u32[]{:S(2)}) copy-start(bf16[512,84]{0,1:T(8,128)(2,1)} %param.23) | copy-start | bytes 258052
  52.6 77.6 %copy-start.4 = (f32[1,2,10752]{2,1,0:T(2,128)S(1)}, f32[1,2,10752]{2,1,0:T(2,128)}, u32[]{:S(2)}) copy-start(f32[1,2,10752]{2,1,0:T(2,128)} %param.13) | copy-start | bytes 258052
  52.6 77.6 %copy-start.6 = (f32[2,10752]{1,0:T(2,128)S(1)}, f32[2,10752]{1,0:T(2,128)}, u32[]{:S(2)}) copy-start(f32[2,10752]{1,0:T(2,128)} %param.14) | copy-start | bytes 258052
Sparse Core Ops, SparseCore 0:
  54.7 60.8 all-gather.1
where the time goes:
time: 215 us; the launch traced here: 214 us
  blocking collectives  73.5 us (34%)
  waiting for transfers between devices  67.5 us (31%)
  other arithmetic  25.9 us (12%)
  between operations  18.1 us (8%)
  local copies, waits for them, and re-layouts  13.1 us (6%)
  matrix products  8.25 us (4%)
  starting transfers between devices  7.01 us (3%)
    psum x1, blocking collectives, local(): change = lax.psum(partial_value, 'band') / (area_total * field_width)  73.5 us
    all_gather x1, waiting for transfers between devices, carried_in(): gathered = lax.all_gather(part, axis)  59.5 us
    add x15, other arithmetic, add_fields(): return earlier + later  14.2 us
    ppermute x1, waiting for transfers between devices, with_halo(): after = lax.ppermute(initial, axis, down)  4.4 us
  transfers between devices with their start and end apart: 4, of which 3 were waited for; matrix products, arithmetic and copies ran while one was open for 2% of the time, Pallas kernels for 0%

commit v1 on v0

v1 whole, which is shorter than its diff:
```python
import math

import jax
import jax.numpy as jnp
import numpy as np
from jax import lax
from jax.experimental import pallas as pl
from jax.experimental.pallas import tpu as pltpu
from jax.sharding import PartitionSpec as P

C = 84
W = 512
HEADS = 4
HEAD_DIM = 128
MLP = 1024
LON = 128
NLAT = 64
LANES = 128
GROUP = 32
SPAN = GROUP * C
PACKS = LON // GROUP
SUB = 2 * PACKS
TILES = SPAN // LANES
TOK = 2 * LON

epsilon = 1e-06
SCORE = 3.0 / math.sqrt(HEAD_DIM)

F32 = jnp.float32
BF16 = jnp.bfloat16


def rms(v):
    return v * lax.rsqrt(jnp.mean(v * v, axis=-1, keepdims=True) + epsilon)


def mm(a, b):
    return jnp.dot(a, b, preferred_element_type=F32)


def to_packed(rows):
    return jnp.concatenate([rows[:, g * SPAN : (g + 1) * SPAN] for g in range(PACKS)], axis=0)


def open_kernel(states_ref, anchor_ref, out_ref):
    last = lax.axis_index("step") == lax.axis_size("step") - 1

    @pl.when(last)
    def _():
        out_ref[...] = to_packed(anchor_ref[...]).astype(BF16)

    @pl.when(jnp.logical_not(last))
    def _():
        out_ref[...] = to_packed(states_ref[0]).astype(BF16)


def unpack_tokens(block_ref, tok_ref):
    lane = lax.broadcasted_iota(jnp.int32, (SUB, LANES), 1)
    x = block_ref[...].astype(F32)
    for r in range(GROUP):
        tile, off = divmod(r * C, LANES)
        v = x[:, tile * LANES : (tile + 1) * LANES]
        if off + C > LANES:
            v = jnp.where(lane >= off, v, x[:, (tile + 1) * LANES : (tile + 2) * LANES])
        if off:
            v = pltpu.roll(v, LANES - off, 1)
        tok_ref[r * SUB : (r + 1) * SUB, :] = v


def denoise_kernel(
    index_ref, sigma_ref, before_ref, here_ref, after_ref, enc_ref, embed_ref, qkv_ref, out_w_ref,
    up_ref, down_ref, dec_ref, drift_ref, drift16_ref, tok_ref,
):
    band = lax.axis_index("band")
    bands = lax.axis_size("band")
    noise = sigma_ref[index_ref[0]]
    offset = jnp.log(jnp.full((1, W), noise, F32)) * embed_ref[...]

    def embed(ref):
        unpack_tokens(ref, tok_ref)
        embedded = mm(tok_ref[...].astype(BF16), enc_ref[...]) + offset
        return embedded, rms(embedded).astype(BF16)

    def heads_of(projected):
        return [
            rms(projected[:, h * HEAD_DIM : (h + 1) * HEAD_DIM]).astype(BF16) for h in range(HEADS)
        ]

    embedded, normed = embed(here_ref)
    queries = heads_of(mm(normed, qkv_ref[:, :W]))
    blocks = [normed, embed(before_ref)[1], embed(after_ref)[1]]
    keys = [heads_of(mm(n, qkv_ref[:, W : 2 * W])) for n in blocks]
    values = [mm(n, qkv_ref[:, 2 * W :]).astype(BF16) for n in blocks]

    q_row = lax.broadcasted_iota(jnp.int32, (TOK, TOK), 0) % 2
    k_row = lax.broadcasted_iota(jnp.int32, (TOK, TOK), 1) % 2
    see_before = (((q_row == 0) | (k_row == 1)) & (band > 0)).astype(F32)
    see_after = (((q_row == 1) | (k_row == 0)) & (band < bands - 1)).astype(F32)
    masks = [None, see_before, see_after]

    attended = []
    for h in range(HEADS):
        total, mix = 0.0, 0.0
        for n in range(3):
            scores = lax.dot_general(
                queries[h], keys[n][h], (((1,), (1,)), ((), ())), preferred_element_type=F32
            )
            weights = jnp.exp(scores * SCORE)
            if masks[n] is not None:
                weights = weights * masks[n]
            total = total + jnp.sum(weights, axis=-1, keepdims=True)
            mix = mix + mm(weights.astype(BF16), values[n][:, h * HEAD_DIM : (h + 1) * HEAD_DIM])
        attended.append((mix / total).astype(BF16))
    attended = jnp.concatenate(attended, axis=1)

    mixed = embedded + mm(attended, out_w_ref[...])
    hidden = jax.nn.gelu(mm(rms(mixed).astype(BF16), up_ref[...])).astype(BF16)
    mixed = mixed + mm(hidden, down_ref[...])
    drift = mm(rms(mixed).astype(BF16), dec_ref[...]) * noise

    lane = lax.broadcasted_iota(jnp.int32, (SUB, LANES), 1)
    tiles = [0.0] * TILES
    for r in range(GROUP):
        tile, off = divmod(r * C, LANES)
        v = drift[r * SUB : (r + 1) * SUB, :]
        if off:
            v = pltpu.roll(v, off, 1)
        if off + C > LANES:
            tiles[tile] = tiles[tile] + jnp.where(lane >= off, v, 0.0)
            tiles[tile + 1] = tiles[tile + 1] + jnp.where(lane < off, v, 0.0)
        else:
            tiles[tile] = tiles[tile] + v
    packed = jnp.concatenate(tiles, axis=1)
    drift_ref[...] = packed
    drift16_ref[...] = packed.astype(BF16)


def close_kernel(area_ref, gathered_ref, drift_ref, anchor_ref, states_ref, new_ref, part_ref):
    step = lax.axis_index("step")
    band = lax.axis_index("band")

    def add(j, total):
        return total + gathered_ref[j].astype(F32)

    earlier = lax.fori_loop(0, step, add, jnp.zeros((SUB, SPAN), F32))
    change = earlier + drift_ref[...]
    row = lax.broadcasted_iota(jnp.int32, (2, 1), 0)
    area = jnp.where(row == 0, area_ref[2 * band], area_ref[2 * band + 1])
    part = jnp.zeros((2, LANES), F32)
    for g in range(PACKS):
        at = slice(g * SPAN, (g + 1) * SPAN)
        new = anchor_ref[:, at] + change[2 * g : 2 * g + 2, :]
        new_ref[0, :, at] = new
        miss = new - states_ref[0, :, at]
        miss = miss * miss
        for t in range(TILES):
            part = part + miss[:, t * LANES : (t + 1) * LANES]
    part = jnp.sum(part * area, axis=0, keepdims=True)
    part_ref[...] = jnp.broadcast_to(part, part_ref.shape)


def local(
    states, anchor, step_index, sigmas, enc_w, noise_embed, qkv_w, out_w, up_w, down_w, dec_w
):
    steps, bands = lax.axis_size("step"), lax.axis_size("band")
    vmem = pl.BlockSpec(memory_space=pltpu.VMEM)
    smem = pl.BlockSpec(memory_space=pltpu.SMEM)
    shape = jax.ShapeDtypeStruct

    block = pl.pallas_call(
        open_kernel, out_shape=shape((SUB, SPAN), BF16), in_specs=[vmem] * 2, out_specs=vmem,
        name="open",
    )(states, anchor)

    def shifted(by):
        pairs = [
            (s * bands + b, ((s + 1) % steps) * bands + b + by)
            for s in range(steps) for b in range(bands) if 0 <= b + by < bands
        ]
        return lax.ppermute(block, ("step", "band"), pairs)

    here, before, after = shifted(0), shifted(1), shifted(-1)
    enc = jnp.pad(enc_w, ((0, LANES - C), (0, 0)))
    dec = jnp.pad(dec_w, ((0, 0), (0, LANES - C)))
    drift, drift16 = pl.pallas_call(
        denoise_kernel,
        out_shape=(shape((SUB, SPAN), F32), shape((SUB, SPAN), BF16)),
        in_specs=[smem] * 2 + [vmem] * 10, out_specs=(vmem, vmem),
        scratch_shapes=[pltpu.VMEM((TOK, LANES), F32)],
        name="denoise",
    )(step_index, sigmas, before, here, after, enc, noise_embed[None], qkv_w, out_w, up_w, down_w, dec)

    gathered = lax.all_gather(drift16, "step")

    latitude = np.pi * ((np.arange(NLAT, dtype=np.float32) + 0.5) / NLAT - 0.5)
    area = np.cos(latitude).astype(np.float32)
    new_states, part = pl.pallas_call(
        close_kernel,
        out_shape=(shape(states.shape, F32), shape((bands, LANES), F32)),
        in_specs=[smem] + [vmem] * 4, out_specs=(vmem, vmem),
        name="close",
    )(jnp.asarray(area), gathered, drift, anchor, states)
    parts = lax.all_to_all(part, "band", 0, 0, tiled=True)
    change = jnp.sum(parts)[None] / (np.float32(area.sum()) * (LON * C))
    return new_states, change


def solution(mesh):
    placed = (
        P("step", "band", None), P("band", None), P("step"), P(), P(), P(), P(), P(), P(), P(), P(),
    )
    return jax.shard_map(
        local,
        mesh=mesh,
        in_specs=placed,
        out_specs=(P("step", "band", None), P("step")),
        check_vma=False,
    )
```

time: 215 us -> 85 us (0.40)
  the two profiles are of different devices: /device:TPU:481 before, /device:TPU:1 now
where the time goes in v1:
time: 85 us; the launch traced here: 84.7 us
  blocking collectives  53 us (62%)
  starting transfers between devices  12.9 us (15%)
  Pallas kernels  10.9 us (13%)
  local copies, waits for them, and re-layouts  3.87 us (5%)
  between operations  3.1 us (4%)
    all_gather x1, blocking collectives, local(): gathered = lax.all_gather(drift16, 'step')  31.9 us
    all_to_all x1, blocking collectives, local(): parts = lax.all_to_all(part, 'band', 0, 0, tiled=True)  21.1 us
    ppermute x3, starting transfers between devices, shifted(): return lax.ppermute(block, ('step', 'band'), pairs)  12.9 us
    pallas_call x1, Pallas kernels, local(): pl.pallas_call(denoise_kernel, out_shape=(shape((SUB, SPAN), F32), shape(...  7.47 us
    pallas_call x1, Pallas kernels, local(): pl.pallas_call(close_kernel, out_shape=(shape(states.shape, F32), shape((...  1.9 us
  transfers between devices with their start and end apart: 3, of which 1 were waited for; matrix products, arithmetic and copies ran while one was open for 4% of the time, Pallas kernels for 0%

profile of v1, /device:TPU:1, one launch (start us, length us, event | category | flops | bytes accessed | tf_op | source)
XLA Modules:
  0.0 84.7 jit_solution(14869423399969913561)
XLA Ops:
  0.6 1.6 %open.1 = bf16[8,2688]{1,0:T(8,128)(2,1)} custom-call(f32[1,2,10752]{2,1,0:T(2,128)} %states_ref.3, f32[2,10752]{1,0:T(2,128)} %anchor_ref.3), custom_call_target="tpu_custom_call" | custom-call | tf_op jit(solution)/shard_map/open/pallas_call | solution.py:170
  2.2 4.9 %collective-permute-start.2 = (bf16[8,2688]{1,0:T(8,128)(2,1)}, bf16[8,2688]{1,0:T(8,128)(2,1)S(1)}, u32[]{:S(2)}, u32[]{:S(2)}) collective-permute-start(bf16[8,2688]{1,0:T(8,128)(2,1)} %open.1), channel_id=1, source_target_pairs={{1,32},{2,33},{3,34},{4,35},{5,36},{6,37},{7,38},{8,39},{9,40},{10... | collective-permute-start | bytes 129032 | tf_op jit(solution)/shard_map/ppermute | solution.py:180
  7.1 3.5 %collective-permute-start.1 = (bf16[8,2688]{1,0:T(8,128)(2,1)}, bf16[8,2688]{1,0:T(8,128)(2,1)S(1)}, u32[]{:S(2)}, u32[]{:S(2)}) collective-permute-start(bf16[8,2688]{1,0:T(8,128)(2,1)} %open.1), channel_id=1, source_target_pairs={{0,32},{1,33},{2,34},{3,35},{4,36},{5,37},{6,38},{7,39},{8,40},{9,... | collective-permute-start | bytes 129032 | tf_op jit(solution)/shard_map/ppermute | solution.py:180
  10.7 4.4 %collective-permute-start = (bf16[8,2688]{1,0:T(8,128)(2,1)}, bf16[8,2688]{1,0:T(8,128)(2,1)S(1)}, u32[]{:S(2)}, u32[]{:S(2)}) collective-permute-start(bf16[8,2688]{1,0:T(8,128)(2,1)} %open.1), channel_id=1, source_target_pairs={{0,33},{1,34},{2,35},{3,36},{4,37},{5,38},{6,39},{7,40},{8,41},{9,... | collective-permute-start | bytes 129032 | tf_op jit(solution)/shard_map/ppermute | solution.py:180
  15.8 1.0 %copy.15 = bf16[512,84]{1,0:T(8,128)(2,1)S(1)} copy(bf16[512,84]{0,1:T(8,128)(2,1)} %param.22) | data formatting | bytes 172032 | tf_op args[10]
  16.8 1.5 %pad.8.enc_ref = bf16[128,512]{1,0:T(8,128)(2,1)} pad(bf16[84,512]{1,0:T(8,128)(2,1)} %param.16, bf16[]{:T(256)} %constant.8.clone.1), padding=0_44x0_0 | pad | bytes 217090 | tf_op jit(solution)/shard_map/jit(_pad)/pad | solution.py:183
  18.4 0.7 pad.9.dec_ref
  19.0 0.0 collective-permute-done.2.after_ref
  19.0 0.0 copy-start
  19.0 0.0 collective-permute-done.1.here_ref
  19.0 0.0 copy-start.1
  19.1 0.2 collective-permute-done.before_ref
  19.3 0.0 copy-start.2
  19.3 0.4 copy-done
  19.7 0.0 copy-done.1
  19.7 0.2 copy-done.2
  19.9 7.5 %denoise.1 = (f32[8,2688]{1,0:T(8,128)}, bf16[8,2688]{1,0:T(8,128)(2,1)}) custom-call(s32[1]{0:T(128)S(6)} %copy.17.index_ref, f32[20]{0:T(128)} %sigma_ref.1, bf16[8,2688]{1,0:T(8,128)(2,1)} %copy-done.2, bf16[8,2688]{1,0:T(8,128)(2,1)} %copy-done.1, bf16[8,2688]{1,0:T(8,128)(2,1)} %copy-done, bf16[128,512]{1,0:T(8,128)(2,1)} %pad.8.enc_ref, ...), custom_call_target="tpu_custom_call" | custom-call | tf_op jit(solution)/shard_map/denoise/pallas_call | solution.py:185
  27.4 31.9 %all-gather = bf16[128,2688]{1,0:T(8,128)(2,1)} all-gather(bf16[8,2688]{1,0:T(8,128)(2,1)} %get-tuple-element.6), channel_id=2, replica_groups=mesh['step'=16,'band'=32] {'step'}, dimensions={0}, use_global_device_ids=true | all-gather | bytes 731136 | tf_op jit(solution)/shard_map/all_gather | solution.py:193
  59.3 1.9 %close.1 = (f32[1,2,10752]{2,1,0:T(2,128)}, f32[32,128]{1,0:T(8,128)}) custom-call(f32[64]{0:T(128)} %constant.11.clone.area_ref, bf16[16,8,2688]{2,1,0:T(8,128)(2,1)} %bitcast.6, f32[8,2688]{1,0:T(8,128)} %get-tuple-element.7.drift_ref, f32[2,10752]{1,0:T(2,128)} %anchor_ref.3, f32[1,2,10752]{2,1,0:T(2,128)} %states_ref.3), custom_call_target="tpu_custom_call" | custom-call | tf_op jit(solution)/shard_map/close/pallas_call | solution.py:197
  61.2 21.1 %all_to_all.9 = f32[32,1,128]{2,1,0:T(1,128)S(1)} all-to-all(f32[32,1,128]{2,1,0:T(1,128)} %bitcast.7), channel_id=1, replica_groups=mesh['step'=16,'band'=32] {'band'}, dimensions={0} | all-to-all | bytes 32768 | tf_op jit(solution)/shard_map/all_to_all | solution.py:203
  82.2 0.6 reduce_sum.9
Async XLA Ops:
  2.2 16.8 %collective-permute-start.2 = (bf16[8,2688]{1,0:T(8,128)(2,1)}, bf16[8,2688]{1,0:T(8,128)(2,1)S(1)}, u32[]{:S(2)}, u32[]{:S(2)}) collective-permute-start(bf16[8,2688]{1,0:T(8,128)(2,1)} %open.1), channel_id=1, source_target_pairs={{1,32},{2,33},{3,34},{4,35},{5,36},{6,37},{7,38},{8,39},{9,40},{10... | collective-permute-start | bytes 129032 | tf_op jit(solution)/shard_map/ppermute | solution.py:180
  7.1 11.9 %collective-permute-start.1 = (bf16[8,2688]{1,0:T(8,128)(2,1)}, bf16[8,2688]{1,0:T(8,128)(2,1)S(1)}, u32[]{:S(2)}, u32[]{:S(2)}) collective-permute-start(bf16[8,2688]{1,0:T(8,128)(2,1)} %open.1), channel_id=1, source_target_pairs={{0,32},{1,33},{2,34},{3,35},{4,36},{5,37},{6,38},{7,39},{8,40},{9,... | collective-permute-start | bytes 129032 | tf_op jit(solution)/shard_map/ppermute | solution.py:180
  10.7 8.6 %collective-permute-start = (bf16[8,2688]{1,0:T(8,128)(2,1)}, bf16[8,2688]{1,0:T(8,128)(2,1)S(1)}, u32[]{:S(2)}, u32[]{:S(2)}) collective-permute-start(bf16[8,2688]{1,0:T(8,128)(2,1)} %open.1), channel_id=1, source_target_pairs={{0,33},{1,34},{2,35},{3,36},{4,37},{5,38},{6,39},{7,40},{8,41},{9,... | collective-permute-start | bytes 129032 | tf_op jit(solution)/shard_map/ppermute | solution.py:180
  19.0 0.6 copy-start
  19.0 0.6 copy-start.1
  19.3 0.6 copy-start.2

commit v2 on v1

v2 whole, which is shorter than its diff:
```python
import math

import jax
import jax.numpy as jnp
import numpy as np
from jax import lax
from jax.experimental import pallas as pl
from jax.experimental.pallas import tpu as pltpu
from jax.sharding import PartitionSpec as P

C = 84
W = 512
HEADS = 4
HEAD_DIM = 128
MLP = 1024
LON = 128
NLAT = 64
LEVELS = 20
LANES = 128
GROUP = 32
SPAN = GROUP * C
PACKS = LON // GROUP
SUB = 2 * PACKS
TILES = SPAN // LANES
TOK = 2 * LON

epsilon = 1e-06
SCORE = 3.0 / math.sqrt(HEAD_DIM)

F32 = jnp.float32
BF16 = jnp.bfloat16


def rms(v):
    return v * lax.rsqrt(jnp.mean(v * v, axis=-1, keepdims=True) + epsilon)


def mm(a, b):
    return jnp.dot(a, b, preferred_element_type=F32)


def to_packed(rows):
    return jnp.concatenate([rows[:, g * SPAN : (g + 1) * SPAN] for g in range(PACKS)], axis=0)


def open_kernel(states_ref, anchor_ref, out_ref, rows_ref):
    last = lax.axis_index("step") == lax.axis_size("step") - 1

    @pl.when(last)
    def _():
        pltpu.sync_copy(anchor_ref, rows_ref)

    @pl.when(jnp.logical_not(last))
    def _():
        pltpu.sync_copy(states_ref.at[0], rows_ref)

    out_ref[...] = to_packed(rows_ref[...]).astype(BF16)


def unpack_tokens(block_ref, tok_ref):
    lane = lax.broadcasted_iota(jnp.int32, (SUB, LANES), 1)
    x = block_ref[...].astype(F32)
    for r in range(GROUP):
        tile, off = divmod(r * C, LANES)
        v = x[:, tile * LANES : (tile + 1) * LANES]
        if off + C > LANES:
            v = jnp.where(lane >= off, v, x[:, (tile + 1) * LANES : (tile + 2) * LANES])
        if off:
            v = pltpu.roll(v, LANES - off, 1)
        tok_ref[r * SUB : (r + 1) * SUB, :] = v


def embed(ref, tok_ref, enc, offset):
    unpack_tokens(ref, tok_ref)
    embedded = mm(tok_ref[...].astype(BF16), enc) + offset
    return embedded, rms(embedded).astype(BF16)


def heads_of(projected):
    return jnp.concatenate(
        [rms(projected[:, h * HEAD_DIM : (h + 1) * HEAD_DIM]) for h in range(HEADS)], axis=1
    ).astype(BF16)


def denoise_kernel(
    noise_ref, here_ref, before_ref, after_ref, offset_ref, enc_hbm, qkv_hbm, out_w_hbm, up_hbm,
    down_hbm, dec_hbm, drift_ref, copies_ref, tok_ref, enc_ref, qkv_ref, out_w_ref, up_ref,
    down_ref, dec_ref, sems,
):
    pairs = (
        (enc_hbm, enc_ref), (qkv_hbm, qkv_ref), (out_w_hbm, out_w_ref), (up_hbm, up_ref),
        (down_hbm, down_ref), (dec_hbm, dec_ref),
    )
    loads = [pltpu.make_async_copy(a, b, sems.at[i]) for i, (a, b) in enumerate(pairs)]
    for load in loads:
        load.start()
    band = lax.axis_index("band")
    bands = lax.axis_size("band")
    noise = noise_ref[0]
    offset = offset_ref[...]

    loads[0].wait()
    enc = jnp.concatenate(
        [enc_ref[...].astype(F32), jnp.zeros((LANES - C, W), F32)], axis=0
    ).astype(BF16)
    embedded, normed = embed(here_ref, tok_ref, enc, offset)
    loads[1].wait()
    queries = heads_of(mm(normed, qkv_ref[:, :W]))
    blocks = [normed]
    blocks += [embed(ref, tok_ref, enc, offset)[1] for ref in (before_ref, after_ref)]
    keys = [heads_of(mm(n, qkv_ref[:, W : 2 * W])) for n in blocks]
    values = [mm(n, qkv_ref[:, 2 * W :]).astype(BF16) for n in blocks]

    q_row = lax.broadcasted_iota(jnp.int32, (TOK, TOK), 0) % 2
    k_row = lax.broadcasted_iota(jnp.int32, (TOK, TOK), 1) % 2
    see_before = (((q_row == 0) | (k_row == 1)) & (band > 0)).astype(F32)
    see_after = (((q_row == 1) | (k_row == 0)) & (band < bands - 1)).astype(F32)
    masks = [None, see_before, see_after]

    attended = []
    for h in range(HEADS):
        at = slice(h * HEAD_DIM, (h + 1) * HEAD_DIM)
        total, mix = 0.0, 0.0
        for n in range(3):
            scores = lax.dot_general(
                queries[:, at], keys[n][:, at], (((1,), (1,)), ((), ())),
                preferred_element_type=F32,
            )
            weights = jnp.exp(scores * SCORE)
            if masks[n] is not None:
                weights = weights * masks[n]
            total = total + jnp.sum(weights, axis=-1, keepdims=True)
            mix = mix + mm(weights.astype(BF16), values[n][:, at])
        attended.append((mix / total).astype(BF16))
    attended = jnp.concatenate(attended, axis=1)

    loads[2].wait()
    mixed = embedded + mm(attended, out_w_ref[...])
    loads[3].wait()
    hidden = jax.nn.gelu(mm(rms(mixed).astype(BF16), up_ref[...])).astype(BF16)
    loads[4].wait()
    mixed = mixed + mm(hidden, down_ref[...])
    loads[5].wait()
    last = rms(mixed).astype(BF16)
    dec = jnp.concatenate([dec_ref[...].astype(F32), jnp.zeros((LANES - C, W), F32)], axis=0)
    drift = noise * lax.dot_general(
        last, dec.astype(BF16), (((1,), (1,)), ((), ())), preferred_element_type=F32
    )

    lane = lax.broadcasted_iota(jnp.int32, (SUB, LANES), 1)
    tiles = [0.0] * TILES
    for r in range(GROUP):
        tile, off = divmod(r * C, LANES)
        v = drift[r * SUB : (r + 1) * SUB, :]
        if off:
            v = pltpu.roll(v, off, 1)
        if off + C > LANES:
            tiles[tile] = tiles[tile] + jnp.where(lane >= off, v, 0.0)
            tiles[tile + 1] = tiles[tile + 1] + jnp.where(lane < off, v, 0.0)
        else:
            tiles[tile] = tiles[tile] + v
    packed = jnp.concatenate(tiles, axis=1)
    drift_ref[...] = packed
    packed = packed.astype(BF16)
    for i in range(4):
        copies_ref[i] = packed


def middle_kernel(group_ref, drift_ref, sent_ref, window_ref):
    place = lax.axis_index("step") % 4
    parts = [group_ref[i].astype(F32) for i in range(4)]
    sent_ref[...] = ((parts[0] + parts[1]) + (parts[2] + parts[3])).astype(BF16)
    window = drift_ref[...]
    for i in range(3):
        window = window + jnp.where(place > i, parts[i], 0.0)
    window_ref[...] = window


def close_kernel(
    area_ref, sum_ref, back4_ref, back8_ref, back12_ref, anchor_ref, states_ref, new_ref, part_ref
):
    band = lax.axis_index("band")
    change = (
        sum_ref[...] + back4_ref[...].astype(F32) + back8_ref[...].astype(F32)
        + back12_ref[...].astype(F32)
    )
    row = lax.broadcasted_iota(jnp.int32, (2, 1), 0)
    area = jnp.where(row == 0, area_ref[2 * band], area_ref[2 * band + 1])
    part = jnp.zeros((2, LANES), F32)
    for g in range(PACKS):
        at = slice(g * SPAN, (g + 1) * SPAN)
        new = anchor_ref[:, at] + change[2 * g : 2 * g + 2, :]
        new_ref[0, :, at] = new
        miss = new - states_ref[0, :, at]
        miss = miss * miss
        for t in range(TILES):
            part = part + miss[:, t * LANES : (t + 1) * LANES]
    part = jnp.sum(part * area, axis=0, keepdims=True)
    part_ref[...] = jnp.broadcast_to(part, part_ref.shape)


def local_vmem(*arrays):
    return [pltpu.with_memory_space_constraint(a, pltpu.VMEM) for a in arrays]


def in_hbm(*arrays):
    return [pltpu.with_memory_space_constraint(a, pltpu.HBM) for a in arrays]


def local(
    states, anchor, step_index, sigmas, enc_w, noise_embed, qkv_w, out_w, up_w, down_w, dec_w
):
    steps, bands = lax.axis_size("step"), lax.axis_size("band")
    vmem = pl.BlockSpec(memory_space=pltpu.VMEM)
    smem = pl.BlockSpec(memory_space=pltpu.SMEM)
    hbm = pl.BlockSpec(memory_space=pltpu.HBM)
    shape = jax.ShapeDtypeStruct

    block = pl.pallas_call(
        open_kernel, out_shape=pltpu.VMEM((SUB, SPAN), BF16), in_specs=[hbm] * 2, out_specs=vmem,
        scratch_shapes=[pltpu.VMEM((2, LON * C), F32)],
        name="open", compiler_params=pltpu.CompilerParams(vmem_limit_bytes=8 << 20),
    )(*in_hbm(states, anchor))

    def later(array, by):
        return lax.ppermute(array, "step", [(s, s + by) for s in range(steps - by)])

    def shifted(by):
        pairs = [
            (s * bands + b, ((s + 1) % steps) * bands + b + by)
            for s in range(steps) for b in range(bands) if 0 <= b + by < bands
        ]
        return lax.ppermute(block, ("step", "band"), pairs)

    here, before, after = shifted(0), shifted(1), shifted(-1)
    onehot = step_index[:, None] == jnp.arange(LEVELS, dtype=jnp.int32)[None, :]
    noise = jnp.sum(jnp.where(onehot, sigmas[None, :], 0.0), axis=1)
    offset = jnp.log(noise)[:, None] * noise_embed[None, :]
    weights = (enc_w, qkv_w, out_w, up_w, down_w, dec_w.T)
    drift, copies = pl.pallas_call(
        denoise_kernel,
        out_shape=(pltpu.VMEM((SUB, SPAN), F32), pltpu.VMEM((4, SUB, SPAN), BF16)),
        in_specs=[smem] + [vmem] * 4 + [hbm] * 6, out_specs=(vmem, vmem),
        scratch_shapes=[pltpu.VMEM((TOK, LANES), F32)]
        + [pltpu.VMEM(w.shape, BF16) for w in weights]
        + [pltpu.SemaphoreType.DMA((len(weights),))],
        name="denoise", compiler_params=pltpu.CompilerParams(vmem_limit_bytes=32 << 20),
    )(noise, *local_vmem(here, before, after, offset), *in_hbm(*weights))

    group = lax.all_to_all(
        copies, "step", 0, 0, tiled=True,
        axis_index_groups=[[4 * g + i for i in range(4)] for g in range(steps // 4)],
    )
    sent, window = pl.pallas_call(
        middle_kernel, out_shape=(pltpu.VMEM((SUB, SPAN), BF16), pltpu.VMEM((SUB, SPAN), F32)),
        in_specs=[vmem] * 2, out_specs=(vmem, vmem), name="middle",
        compiler_params=pltpu.CompilerParams(vmem_limit_bytes=8 << 20),
    )(*local_vmem(group, drift))
    far = [later(sent, by) for by in (4, 8, 12)]

    latitude = np.pi * ((np.arange(NLAT, dtype=np.float32) + 0.5) / NLAT - 0.5)
    area = np.cos(latitude).astype(np.float32)
    new_states, part = pl.pallas_call(
        close_kernel,
        out_shape=(shape(states.shape, F32), pltpu.VMEM((bands, LANES), F32)),
        in_specs=[smem] + [vmem] * 6, out_specs=(vmem, vmem),
        name="close", compiler_params=pltpu.CompilerParams(vmem_limit_bytes=16 << 20),
    )(jnp.asarray(area), *local_vmem(window, *far, anchor, states))
    parts = lax.all_to_all(part, "band", 0, 0, tiled=True)
    change = jnp.sum(parts)[None] / (np.float32(area.sum()) * (LON * C))
    return new_states, change


def solution(mesh):
    placed = (
        P("step", "band", None), P("band", None), P("step"), P(), P(), P(), P(), P(), P(), P(), P(),
    )
    return jax.shard_map(
        local,
        mesh=mesh,
        in_specs=placed,
        out_specs=(P("step", "band", None), P("step")),
        check_vma=False,
    )
```

time: 85 us -> 73.5 us (0.86)
  blocking collectives: 53 us -> 28.5 us
  starting transfers between devices: 12.9 us -> 26.6 us
  local copies, waits for them, and re-layouts: 3.87 us -> 0.01 us
  waiting for transfers between devices: 0.22 us -> 2.4 us
  other arithmetic: 0.63 us -> 2.58 us
  Pallas kernels: 10.9 us -> 9.11 us
    all_gather x1 -> x0, blocking collectives: 31.9 us -> none  [local(): gathered = lax.all_gather(drift16, 'step')]
    ppermute x0 -> x3, starting transfers between devices: none -> 14 us  [later(): return lax.ppermute(array, 'step', [(s, s + by) for s in range(steps - by)])]
    all_to_all x0 -> x1, blocking collectives: none -> 11.6 us  [local(): lax.all_to_all(copies, 'step', 0, 0, tiled=True, axis_index_groups=[[4 *...]
    all_to_all x1, blocking collectives: 21.1 us -> 16.9 us  [local(): parts = lax.all_to_all(part, 'band', 0, 0, tiled=True)]
    pad x2 -> x0, local copies, waits for them, and re-layouts: 2.22 us -> none  [the longest x1 1.54 us: local(): enc = jnp.pad(enc_w, ((0, LANES - C), (0, 0)))]
    pallas_call x3 -> x4, Pallas kernels: 10.9 us -> 9.11 us  [the longest x1 6.9 us: local(): pl.pallas_call(denoise_kernel, out_shape=(pltpu.VMEM((SUB, SPAN), F32), p...]
    unnamed x7 -> x6, local copies, waits for them, and re-layouts: 1.65 us -> 0.01 us
    reduce_sum x0 -> x1, other arithmetic: none -> 1.26 us  [local(): noise = jnp.sum(jnp.where(onehot, sigmas[None, :], 0.0), axis=1)]
  transfers between devices with their start and end apart: 3 -> 6, of which waited for: 1 -> 2; matrix products, arithmetic and copies ran while one was open for 4% -> 3% of each run, Pallas kernels for 0% -> 0%
where the time goes in v2:
time: 73.5 us; the launch traced here: 73.1 us
  blocking collectives  28.5 us (39%)
  starting transfers between devices  26.6 us (36%)
  Pallas kernels  9.11 us (12%)
  between operations  3.83 us (5%)
  other arithmetic  2.58 us (4%)
  waiting for transfers between devices  2.4 us (3%)
    all_to_all x1, blocking collectives, local(): parts = lax.all_to_all(part, 'band', 0, 0, tiled=True)  16.9 us
    ppermute x3, starting transfers between devices, later(): return lax.ppermute(array, 'step', [(s, s + by) for s in range(steps - by)])  14 us
    ppermute x3, starting transfers between devices, shifted(): return lax.ppermute(block, ('step', 'band'), pairs)  12.6 us
    all_to_all x1, blocking collectives, local(): lax.all_to_all(copies, 'step', 0, 0, tiled=True, axis_index_groups=[[4 *...  11.6 us
    pallas_call x1, Pallas kernels, local(): pl.pallas_call(denoise_kernel, out_shape=(pltpu.VMEM((SUB, SPAN), F32), p...  6.9 us
  transfers between devices with their start and end apart: 6, of which 2 were waited for; matrix products, arithmetic and copies ran while one was open for 3% of the time, Pallas kernels for 0%

profile of v2, /device:TPU:1, one launch (start us, length us, event | category | flops | bytes accessed | tf_op | source)
XLA Modules:
  0.0 73.1 jit_solution(2730940501166510937)
XLA Ops:
  0.6 0.9 %open.1 = bf16[8,2688]{1,0:T(8,128)(2,1)S(1)} custom-call(f32[1,2,10752]{2,1,0:T(2,128)} %states_ref.3, f32[2,10752]{1,0:T(2,128)} %anchor_ref.3), custom_call_target="tpu_custom_call" | custom-call | tf_op jit(solution)/shard_map/open/pallas_call | solution.py:219
  1.6 4.9 %collective-permute-start.2 = (bf16[8,2688]{1,0:T(8,128)(2,1)S(1)}, bf16[8,2688]{1,0:T(8,128)(2,1)S(1)}, u32[]{:S(2)}, u32[]{:S(2)}) collective-permute-start(bf16[8,2688]{1,0:T(8,128)(2,1)S(1)} %open.1), channel_id=1, source_target_pairs={{1,32},{2,33},{3,34},{4,35},{5,36},{6,37},{7,38},{8,39},{9,40},{10... | collective-permute-start | bytes 129032 | tf_op jit(solution)/shard_map/ppermute | solution.py:233
  6.5 4.2 %collective-permute-start.1 = (bf16[8,2688]{1,0:T(8,128)(2,1)S(1)}, bf16[8,2688]{1,0:T(8,128)(2,1)S(1)}, u32[]{:S(2)}, u32[]{:S(2)}) collective-permute-start(bf16[8,2688]{1,0:T(8,128)(2,1)S(1)} %open.1), channel_id=1, source_target_pairs={{0,33},{1,34},{2,35},{3,36},{4,37},{5,38},{6,39},{7,40},{8,41},{9,... | collective-permute-start | bytes 129032 | tf_op jit(solution)/shard_map/ppermute | solution.py:233
  10.7 3.5 %collective-permute-start = (bf16[8,2688]{1,0:T(8,128)(2,1)S(1)}, bf16[8,2688]{1,0:T(8,128)(2,1)S(1)}, u32[]{:S(2)}, u32[]{:S(2)}) collective-permute-start(bf16[8,2688]{1,0:T(8,128)(2,1)S(1)} %open.1), channel_id=1, source_target_pairs={{0,32},{1,33},{2,34},{3,35},{4,36},{5,37},{6,38},{7,39},{8,40},{9,... | collective-permute-start | bytes 129032 | tf_op jit(solution)/shard_map/ppermute | solution.py:233
  14.9 1.3 %fusion = f32[]{:T(128)} fusion(f32[20]{0:T(128)} %param.15, s32[]{:T(128)} %bitcast.9), kind=kLoop, calls=%fused_computation.2 | loop fusion | flops 59 | bytes 88 | tf_op jit(solution)/shard_map/reduce_sum | solution.py:237
  16.8 0.7 broadcast_multiply_fusion
  17.5 0.0 collective-permute-done.2.after_ref
  17.5 0.0 collective-permute-done.1.before_ref
  17.5 1.3 %collective-permute-done.here_ref = bf16[8,2688]{1,0:T(8,128)(2,1)S(1)} collective-permute-done((bf16[8,2688]{1,0:T(8,128)(2,1)S(1)}, bf16[8,2688]{1,0:T(8,128)(2,1)S(1)}, u32[]{:S(2)}, u32[]{:S(2)}) %collective-permute-start) | collective-permute-done | bytes 43040 | tf_op jit(solution)/shard_map/ppermute | solution.py:233
  18.8 0.0 copy-start
  18.8 0.0 copy-start.1
  18.8 0.0 copy-start.2
  18.8 6.9 %denoise.1 = (f32[8,2688]{1,0:T(8,128)S(1)}, bf16[4,8,2688]{2,1,0:T(8,128)(2,1)S(1)}) custom-call(f32[1]{0:T(128)} %bitcast.1.noise_ref, bf16[8,2688]{1,0:T(8,128)(2,1)S(1)} %collective-permute-done.here_ref, bf16[8,2688]{1,0:T(8,128)(2,1)S(1)} %collective-permute-done.1.before_ref, bf16[8,2688]{1,0:T(8,128)(2,1)S(1)} %collective-permute-done.2.after_ref, ...), custom_call_target="tpu_custom_call" | custom-call | tf_op jit(solution)/shard_map/denoise/pallas_call | solution.py:240
  25.7 11.6 %all_to_all.14.group_ref = bf16[4,8,2688]{2,1,0:T(8,128)(2,1)S(1)} all-to-all(bf16[4,8,2688]{2,1,0:T(8,128)(2,1)S(1)} %get-tuple-element.8), channel_id=1, replica_groups={{0,32,64,96},{128,160,192,224},{256,288,320,352},{384,416,448,480},{1,3..., dimensions={0} | all-to-all | bytes 344064 | tf_op jit(solution)/shard_map/all_to_all | solution.py:250
  37.4 5.7 %collective-permute-start.5 = (bf16[8,2688]{1,0:T(8,128)(2,1)S(1)}, bf16[8,2688]{1,0:T(8,128)(2,1)S(1)}, u32[]{:S(2)}, u32[]{:S(2)}) collective-permute-start(bf16[8,2688]{1,0:T(8,128)(2,1)S(1)} %get-tuple-element.11), channel_id=1, source_target_pairs={{0,384},{32,416},{64,448},{96,480},{1,385},{33,417},{65,449},{97,4... | collective-permute-start | bytes 129032 | tf_op jit(solution)/shard_map/ppermute | solution.py:226
  43.1 3.6 %collective-permute-start.4 = (bf16[8,2688]{1,0:T(8,128)(2,1)S(1)}, bf16[8,2688]{1,0:T(8,128)(2,1)S(1)}, u32[]{:S(2)}, u32[]{:S(2)}) collective-permute-start(bf16[8,2688]{1,0:T(8,128)(2,1)S(1)} %get-tuple-element.11), channel_id=1, source_target_pairs={{0,256},{32,288},{64,320},{96,352},{128,384},{160,416},{192,448},{... | collective-permute-start | bytes 129032 | tf_op jit(solution)/shard_map/ppermute | solution.py:226
  46.8 4.6 %collective-permute-start.3 = (bf16[8,2688]{1,0:T(8,128)(2,1)S(1)}, bf16[8,2688]{1,0:T(8,128)(2,1)S(1)}, u32[]{:S(2)}, u32[]{:S(2)}) collective-permute-start(bf16[8,2688]{1,0:T(8,128)(2,1)S(1)} %get-tuple-element.11), channel_id=1, source_target_pairs={{0,128},{32,160},{64,192},{96,224},{128,256},{160,288},{192,320},{... | collective-permute-start | bytes 129032 | tf_op jit(solution)/shard_map/ppermute | solution.py:226
  51.4 0.0 collective-permute-done.5.back12_ref
  51.4 0.0 collective-permute-done.4.back8_ref
  51.4 1.1 %collective-permute-done.3.back4_ref = bf16[8,2688]{1,0:T(8,128)(2,1)S(1)} collective-permute-done((bf16[8,2688]{1,0:T(8,128)(2,1)S(1)}, bf16[8,2688]{1,0:T(8,128)(2,1)S(1)}, u32[]{:S(2)}, u32[]{:S(2)}) %collective-permute-start.3) | collective-permute-done | bytes 43040 | tf_op jit(solution)/shard_map/ppermute | solution.py:226
  52.5 0.0 copy-done
  52.5 0.0 copy-done.1
  52.5 0.0 copy-done.2
  52.5 1.2 %close.1 = (f32[1,2,10752]{2,1,0:T(2,128)}, f32[32,128]{1,0:T(8,128)S(1)}) custom-call(f32[64]{0:T(128)S(1)} %copy-done.2, f32[8,2688]{1,0:T(8,128)S(1)} %get-tuple-element.10.sum_ref, bf16[8,2688]{1,0:T(8,128)(2,1)S(1)} %collective-permute-done.3.back4_ref, bf16[8,2688]{1,0:T(8,128)(2,1)S(1)} %collective-permute-done.4.back8_ref, ...), custom_call_target="tpu_custom_call" | custom-call | tf_op jit(solution)/shard_map/close/pallas_call | solution.py:263
  53.7 16.9 %all_to_all.15 = f32[32,1,128]{2,1,0:T(1,128)S(1)} all-to-all(f32[32,1,128]{2,1,0:T(1,128)S(1)} %bitcast.10), channel_id=1, replica_groups=mesh['step'=16,'band'=32] {'band'}, dimensions={0} | all-to-all | bytes 32768 | tf_op jit(solution)/shard_map/all_to_all | solution.py:269
  70.7 0.6 reduce_sum.22
  (1 shorter events, 0.0 us)
Async XLA Ops:
  1.6 15.9 %collective-permute-start.2 = (bf16[8,2688]{1,0:T(8,128)(2,1)S(1)}, bf16[8,2688]{1,0:T(8,128)(2,1)S(1)}, u32[]{:S(2)}, u32[]{:S(2)}) collective-permute-start(bf16[8,2688]{1,0:T(8,128)(2,1)S(1)} %open.1), channel_id=1, source_target_pairs={{1,32},{2,33},{3,34},{4,35},{5,36},{6,37},{7,38},{8,39},{9,40},{10... | collective-permute-start | bytes 129032 | tf_op jit(solution)/shard_map/ppermute | solution.py:233
  6.5 11.0 %collective-permute-start.1 = (bf16[8,2688]{1,0:T(8,128)(2,1)S(1)}, bf16[8,2688]{1,0:T(8,128)(2,1)S(1)}, u32[]{:S(2)}, u32[]{:S(2)}) collective-permute-start(bf16[8,2688]{1,0:T(8,128)(2,1)S(1)} %open.1), channel_id=1, source_target_pairs={{0,33},{1,34},{2,35},{3,36},{4,37},{5,38},{6,39},{7,40},{8,41},{9,... | collective-permute-start | bytes 129032 | tf_op jit(solution)/shard_map/ppermute | solution.py:233
  10.7 8.2 %collective-permute-start = (bf16[8,2688]{1,0:T(8,128)(2,1)S(1)}, bf16[8,2688]{1,0:T(8,128)(2,1)S(1)}, u32[]{:S(2)}, u32[]{:S(2)}) collective-permute-start(bf16[8,2688]{1,0:T(8,128)(2,1)S(1)} %open.1), channel_id=1, source_target_pairs={{0,32},{1,33},{2,34},{3,35},{4,36},{5,37},{6,38},{7,39},{8,40},{9,... | collective-permute-start | bytes 129032 | tf_op jit(solution)/shard_map/ppermute | solution.py:233
  18.8 33.7 %copy-start = (f32[1,2,10752]{2,1,0:T(2,128)S(1)}, f32[1,2,10752]{2,1,0:T(2,128)}, u32[]{:S(2)}) copy-start(f32[1,2,10752]{2,1,0:T(2,128)} %states_ref.3) | copy-start | bytes 258052
  18.8 33.7 %copy-start.1 = (f32[2,10752]{1,0:T(2,128)S(1)}, f32[2,10752]{1,0:T(2,128)}, u32[]{:S(2)}) copy-start(f32[2,10752]{1,0:T(2,128)} %anchor_ref.3) | copy-start | bytes 258052
  18.8 33.7 %copy-start.2 = (f32[64]{0:T(128)S(1)}, f32[64]{0:T(128)}, u32[]{:S(2)}) copy-start(f32[64]{0:T(128)} %constant.8.clone.area_ref) | copy-start | bytes 772
  37.4 14.0 %collective-permute-start.5 = (bf16[8,2688]{1,0:T(8,128)(2,1)S(1)}, bf16[8,2688]{1,0:T(8,128)(2,1)S(1)}, u32[]{:S(2)}, u32[]{:S(2)}) collective-permute-start(bf16[8,2688]{1,0:T(8,128)(2,1)S(1)} %get-tuple-element.11), channel_id=1, source_target_pairs={{0,384},{32,416},{64,448},{96,480},{1,385},{33,417},{65,449},{97,4... | collective-permute-start | bytes 129032 | tf_op jit(solution)/shard_map/ppermute | solution.py:226
  43.1 8.3 %collective-permute-start.4 = (bf16[8,2688]{1,0:T(8,128)(2,1)S(1)}, bf16[8,2688]{1,0:T(8,128)(2,1)S(1)}, u32[]{:S(2)}, u32[]{:S(2)}) collective-permute-start(bf16[8,2688]{1,0:T(8,128)(2,1)S(1)} %get-tuple-element.11), channel_id=1, source_target_pairs={{0,256},{32,288},{64,320},{96,352},{128,384},{160,416},{192,448},{... | collective-permute-start | bytes 129032 | tf_op jit(solution)/shard_map/ppermute | solution.py:226
  46.8 5.8 %collective-permute-start.3 = (bf16[8,2688]{1,0:T(8,128)(2,1)S(1)}, bf16[8,2688]{1,0:T(8,128)(2,1)S(1)}, u32[]{:S(2)}, u32[]{:S(2)}) collective-permute-start(bf16[8,2688]{1,0:T(8,128)(2,1)S(1)} %get-tuple-element.11), channel_id=1, source_target_pairs={{0,128},{32,160},{64,192},{96,224},{128,256},{160,288},{192,320},{... | collective-permute-start | bytes 129032 | tf_op jit(solution)/shard_map/ppermute | solution.py:226

commit v3 on v2

v3 whole, which is shorter than its diff:
```python
import math

import jax
import jax.numpy as jnp
import numpy as np
from jax import lax
from jax.experimental import pallas as pl
from jax.experimental.pallas import tpu as pltpu
from jax.sharding import PartitionSpec as P

C = 84
W = 512
HEADS = 4
HEAD_DIM = 128
LON = 128
NLAT = 64
LEVELS = 20
LANES = 128
GROUP = 32
SPAN = GROUP * C
PACKS = LON // GROUP
SUB = 2 * PACKS
TILES = SPAN // LANES
TOK = 2 * LON

FAR = (
    [(2, 3), (0, 4), (1, 5), (15, 6)] + [(s, s + 4) for s in range(3, 11)] + [(14, 15)],
    [(2, 7), (1, 8), (0, 9), (15, 10), (6, 11), (5, 12), (4, 13), (3, 14), (10, 15)],
    [(15, 11), (0, 12), (1, 13), (2, 14), (3, 15)],
)

epsilon = 1e-06
SCORE = 3.0 / math.sqrt(HEAD_DIM)

F32 = jnp.float32
BF16 = jnp.bfloat16


def rms(v):
    return v * lax.rsqrt(jnp.mean(v * v, axis=-1, keepdims=True) + epsilon)


def mm(a, b):
    return jnp.dot(a, b, preferred_element_type=F32)


def to_packed(rows):
    return jnp.concatenate([rows[:, g * SPAN : (g + 1) * SPAN] for g in range(PACKS)], axis=0)


def open_kernel(states_ref, anchor_ref, out_ref, rows_ref):
    last = lax.axis_index("step") == lax.axis_size("step") - 1

    @pl.when(last)
    def _():
        pltpu.sync_copy(anchor_ref, rows_ref)

    @pl.when(jnp.logical_not(last))
    def _():
        pltpu.sync_copy(states_ref.at[0], rows_ref)

    out_ref[...] = to_packed(rows_ref[...]).astype(BF16)


def unpack_tokens(block_ref, tok_ref):
    lane = lax.broadcasted_iota(jnp.int32, (SUB, LANES), 1)
    x = block_ref[...].astype(F32)
    for r in range(GROUP):
        tile, off = divmod(r * C, LANES)
        v = x[:, tile * LANES : (tile + 1) * LANES]
        if off + C > LANES:
            v = jnp.where(lane >= off, v, x[:, (tile + 1) * LANES : (tile + 2) * LANES])
        if off:
            v = pltpu.roll(v, LANES - off, 1)
        tok_ref[r * SUB : (r + 1) * SUB, :] = v


def embed(ref, tok_ref, enc_ref, offset):
    unpack_tokens(ref, tok_ref)
    enc = jnp.concatenate(
        [enc_ref[...].astype(F32), jnp.zeros((LANES - C, W), F32)], axis=0
    ).astype(BF16)
    embedded = mm(tok_ref[...].astype(BF16), enc) + offset
    return embedded, rms(embedded).astype(BF16)


def heads_of(projected):
    return jnp.concatenate(
        [rms(projected[:, h * HEAD_DIM : (h + 1) * HEAD_DIM]) for h in range(HEADS)], axis=1
    ).astype(BF16)


def own_kernel(
    index_ref, sigma_ref, embed_ref, here_ref, enc_ref, qkv_ref, embedded_ref, heads_ref,
    offset_ref, noise_ref, tok_ref,
):
    level = lax.broadcasted_iota(jnp.int32, (1, LEVELS), 1)
    noise = jnp.sum(
        jnp.where(level == index_ref[...], sigma_ref[...], 0.0), axis=1, keepdims=True
    )
    offset = jnp.log(noise) * embed_ref[...]
    offset_ref[...] = offset
    noise_ref[...] = jnp.broadcast_to(noise, noise_ref.shape)
    embedded, normed = embed(here_ref, tok_ref, enc_ref, offset)
    embedded_ref[...] = embedded
    heads_ref[0] = heads_of(mm(normed, qkv_ref[:, :W]))
    heads_ref[1] = heads_of(mm(normed, qkv_ref[:, W : 2 * W]))
    heads_ref[2] = mm(normed, qkv_ref[:, 2 * W :]).astype(BF16)


def denoise_kernel(
    before_ref, after_ref, embedded_ref, heads_ref, offset_ref, noise_ref, enc_ref, qkv_ref,
    out_w_ref, up_ref, down_ref, dec_ref, copies_ref, tok_ref,
):
    band = lax.axis_index("band")
    bands = lax.axis_size("band")
    offset = offset_ref[...]
    blocks = [embed(ref, tok_ref, enc_ref, offset)[1] for ref in (before_ref, after_ref)]
    queries = heads_ref[0]
    keys = [heads_ref[1]] + [heads_of(mm(n, qkv_ref[:, W : 2 * W])) for n in blocks]
    values = [heads_ref[2]] + [mm(n, qkv_ref[:, 2 * W :]).astype(BF16) for n in blocks]

    q_row = lax.broadcasted_iota(jnp.int32, (TOK, TOK), 0) % 2
    k_row = lax.broadcasted_iota(jnp.int32, (TOK, TOK), 1) % 2
    see_before = (((q_row == 0) | (k_row == 1)) & (band > 0)).astype(F32)
    see_after = (((q_row == 1) | (k_row == 0)) & (band < bands - 1)).astype(F32)
    masks = [None, see_before, see_after]

    attended = []
    for h in range(HEADS):
        at = slice(h * HEAD_DIM, (h + 1) * HEAD_DIM)
        total, mix = 0.0, 0.0
        for n in range(3):
            scores = lax.dot_general(
                queries[:, at], keys[n][:, at], (((1,), (1,)), ((), ())),
                preferred_element_type=F32,
            )
            weights = jnp.exp(scores * SCORE)
            if masks[n] is not None:
                weights = weights * masks[n]
            total = total + jnp.sum(weights, axis=-1, keepdims=True)
            mix = mix + mm(weights.astype(BF16), values[n][:, at])
        attended.append((mix / total).astype(BF16))
    attended = jnp.concatenate(attended, axis=1)

    mixed = embedded_ref[...] + mm(attended, out_w_ref[...])
    hidden = jax.nn.gelu(mm(rms(mixed).astype(BF16), up_ref[...])).astype(BF16)
    mixed = mixed + mm(hidden, down_ref[...])
    last = rms(mixed).astype(BF16)
    dec = jnp.concatenate([dec_ref[...].astype(F32), jnp.zeros((LANES - C, W), F32)], axis=0)
    drift = noise_ref[...] * lax.dot_general(
        last, dec.astype(BF16), (((1,), (1,)), ((), ())), preferred_element_type=F32
    )

    lane = lax.broadcasted_iota(jnp.int32, (SUB, LANES), 1)
    tiles = [0.0] * TILES
    for r in range(GROUP):
        tile, off = divmod(r * C, LANES)
        v = drift[r * SUB : (r + 1) * SUB, :]
        if off:
            v = pltpu.roll(v, off, 1)
        if off + C > LANES:
            tiles[tile] = tiles[tile] + jnp.where(lane >= off, v, 0.0)
            tiles[tile + 1] = tiles[tile + 1] + jnp.where(lane < off, v, 0.0)
        else:
            tiles[tile] = tiles[tile] + v
    packed = jnp.concatenate(tiles, axis=1)
    packed = packed.astype(BF16)
    for i in range(4):
        copies_ref[i] = packed


def middle_kernel(group_ref, sent_ref):
    parts = [group_ref[i].astype(F32) for i in range(4)]
    sent_ref[...] = ((parts[0] + parts[1]) + (parts[2] + parts[3])).astype(BF16)


def base_kernel(group_ref, anchor_ref, states_ref, area_ref, base_ref, old_ref, scale_ref):
    step = lax.axis_index("step")
    band = lax.axis_index("band")
    last = step == lax.axis_size("step") - 1
    place = jnp.where(last, 4, (step + 1) % 4)
    window = jnp.where(place > 0, group_ref[0].astype(F32), 0.0)
    for i in range(1, 4):
        window = window + jnp.where(place > i, group_ref[i].astype(F32), 0.0)
    base_ref[...] = to_packed(anchor_ref[...]) + window
    old_ref[...] = to_packed(states_ref[0])
    row = 2 * band + lax.broadcasted_iota(jnp.int32, (SUB, NLAT), 0) % 2
    pick = lax.broadcasted_iota(jnp.int32, (SUB, NLAT), 1) == row
    area = jnp.sum(jnp.where(pick, area_ref[...], 0.0), axis=1, keepdims=True)
    scale_ref[...] = jnp.broadcast_to(area, scale_ref.shape)


def close_kernel(
    back4_ref, back8_ref, back12_ref, base_ref, old_ref, scale_ref, new_ref, part_ref
):
    new = base_ref[...] + (
        back4_ref[...].astype(F32) + back8_ref[...].astype(F32) + back12_ref[...].astype(F32)
    )
    for g in range(PACKS):
        new_ref[0, :, g * SPAN : (g + 1) * SPAN] = new[2 * g : 2 * g + 2, :]
    miss = new - old_ref[...]
    miss = miss * miss
    part = miss[:, :LANES]
    for t in range(1, TILES):
        part = part + miss[:, t * LANES : (t + 1) * LANES]
    part = jnp.sum(part * scale_ref[...], axis=0, keepdims=True)
    part_ref[...] = jnp.broadcast_to(part, part_ref.shape)


def local_vmem(*arrays):
    return [pltpu.with_memory_space_constraint(a, pltpu.VMEM) for a in arrays]


def in_hbm(*arrays):
    return [pltpu.with_memory_space_constraint(a, pltpu.HBM) for a in arrays]


def local(
    states, anchor, step_index, sigmas, enc_w, noise_embed, qkv_w, out_w, up_w, down_w, dec_w
):
    steps, bands = lax.axis_size("step"), lax.axis_size("band")
    vmem = pl.BlockSpec(memory_space=pltpu.VMEM)
    smem = pl.BlockSpec(memory_space=pltpu.SMEM)
    hbm = pl.BlockSpec(memory_space=pltpu.HBM)

    block = pl.pallas_call(
        open_kernel, out_shape=pltpu.VMEM((SUB, SPAN), BF16), in_specs=[hbm] * 2, out_specs=vmem,
        scratch_shapes=[pltpu.VMEM((2, LON * C), F32)],
        cost_estimate=pl.CostEstimate(flops=10**10, bytes_accessed=10**6, transcendentals=0),
        name="open", compiler_params=pltpu.CompilerParams(vmem_limit_bytes=8 << 20),
    )(*in_hbm(states, anchor))

    index = lax.ppermute(step_index, "step", [((s + 1) % steps, s) for s in range(steps)])
    before = lax.ppermute(block, "band", [(b, b + 1) for b in range(bands - 1)])
    after = lax.ppermute(block, "band", [(b + 1, b) for b in range(bands - 1)])

    def limit(mib):
        return pltpu.CompilerParams(vmem_limit_bytes=mib << 20)

    tokens = pltpu.VMEM((TOK, LANES), F32)
    own = pl.pallas_call(
        own_kernel,
        out_shape=(
            pltpu.VMEM((TOK, W), F32), pltpu.VMEM((3, TOK, W), BF16), pltpu.VMEM((1, W), F32),
            pltpu.VMEM((1, LANES), F32),
        ),
        in_specs=[vmem] * 6, out_specs=(vmem,) * 4, scratch_shapes=[tokens],
        name="own", compiler_params=limit(16),
    )(*local_vmem(index[None], sigmas[None], noise_embed[None], block, enc_w, qkv_w))
    copies = pl.pallas_call(
        denoise_kernel,
        out_shape=pltpu.VMEM((4, SUB, SPAN), BF16),
        in_specs=[vmem] * 12, out_specs=vmem, scratch_shapes=[tokens],
        name="denoise", compiler_params=limit(32),
    )(*local_vmem(before, after, *own, enc_w, qkv_w, out_w, up_w, down_w, dec_w.T))

    group = lax.all_to_all(
        copies, "step", 0, 0, tiled=True,
        axis_index_groups=[[(4 * g + i - 1) % steps for i in range(4)] for g in range(steps // 4)],
    )
    packed = pltpu.VMEM((SUB, SPAN), F32)
    sent = pl.pallas_call(
        middle_kernel, out_shape=pltpu.VMEM((SUB, SPAN), BF16), in_specs=[vmem], out_specs=vmem,
        name="middle", compiler_params=limit(8),
    )(*local_vmem(group))
    far = []
    for pairs in FAR:
        far.append(lax.ppermute(sent, "step", pairs))
    latitude = np.pi * ((np.arange(NLAT, dtype=np.float32) + 0.5) / NLAT - 0.5)
    area = np.cos(latitude).astype(np.float32)
    base = pl.pallas_call(
        base_kernel, out_shape=(packed, packed, pltpu.VMEM((SUB, LANES), F32)),
        in_specs=[vmem] * 4, out_specs=(vmem,) * 3, name="base", compiler_params=limit(8),
    )(*local_vmem(group, anchor, states, jnp.asarray(area)[None]))
    new_states, part = pl.pallas_call(
        close_kernel,
        out_shape=(pltpu.VMEM(states.shape, F32), pltpu.VMEM((bands, LANES), F32)),
        in_specs=[vmem] * 6, out_specs=(vmem, vmem), name="close", compiler_params=limit(8),
    )(*local_vmem(*far, *base))
    parts = lax.all_to_all(part, "band", 0, 0, tiled=True)
    change = jnp.sum(parts)[None] / (np.float32(area.sum()) * (LON * C))
    return new_states, change


def solution(mesh):
    placed = (
        P("step", "band", None), P("band", None), P("step"), P(), P(), P(), P(), P(), P(), P(), P(),
    )
    return jax.shard_map(
        local,
        mesh=mesh,
        in_specs=placed,
        out_specs=(P("step", "band", None), P("step")),
        check_vma=False,
    )
```

time: 73.5 us -> 70.8 us (0.963)
  blocking collectives: 28.5 us -> 10.6 us
  starting transfers between devices: 26.6 us -> 39.8 us
  waiting for transfers between devices: 2.4 us -> 8.07 us
  other arithmetic: 2.58 us -> 0.63 us
  Pallas kernels: 9.11 us -> 7.55 us
  between operations: 3.83 us -> 2.65 us
    all_to_all x2 -> x1, blocking collectives: 28.5 us -> 10.6 us  [local(): lax.all_to_all(copies, 'step', 0, 0, tiled=True, axis_index_groups=[[(4 *...]
    all_to_all x0 -> x1, starting transfers between devices: none -> 9.08 us  [local(): parts = lax.all_to_all(part, 'band', 0, 0, tiled=True)]
    all_to_all x0 -> x1, waiting for transfers between devices: none -> 6.33 us  [local(): parts = lax.all_to_all(part, 'band', 0, 0, tiled=True)]
    ppermute x6, starting transfers between devices: 26.6 us -> 30.7 us  [the longest x3 12.9 us: local(): far.append(lax.ppermute(sent, 'step', pairs))]
    pallas_call x3 -> x5, Pallas kernels: 8.17 us -> 6.47 us  [the longest x1 4.05 us: local(): pl.pallas_call(denoise_kernel, out_shape=pltpu.VMEM((4, SUB, SPAN), BF16)...]
    reduce_sum x1 -> x0, other arithmetic: 1.26 us -> none  [local(): noise = jnp.sum(jnp.where(onehot, sigmas[None, :], 0.0), axis=1)]
  transfers between devices with their start and end apart: 6 -> 7, of which waited for: 2 -> 3; matrix products, arithmetic and copies ran while one was open for 3% -> 1% of each run, Pallas kernels for 0% -> 2%
where the time goes in v3:
time: 70.8 us; the launch traced here: 70 us
  starting transfers between devices  39.8 us (56%)
  blocking collectives  10.6 us (15%)
  waiting for transfers between devices  8.07 us (11%)
  Pallas kernels  7.55 us (11%)
  between operations  2.65 us (4%)
    ppermute x3, starting transfers between devices, local(): far.append(lax.ppermute(sent, 'step', pairs))  12.9 us
    all_to_all x1, blocking collectives, local(): lax.all_to_all(copies, 'step', 0, 0, tiled=True, axis_index_groups=[[(4 *...  10.6 us
    all_to_all x1, starting transfers between devices, local(): parts = lax.all_to_all(part, 'band', 0, 0, tiled=True)  9.08 us
    ppermute x1, starting transfers between devices, local(): after = lax.ppermute(block, 'band', [(b + 1, b) for b in range(bands - 1)])  8.88 us
    ppermute x1, starting transfers between devices, local(): lax.ppermute(step_index, 'step', [((s + 1) % steps, s) for s in range(ste...  6.96 us
    all_to_all x1, waiting for transfers between devices, local(): parts = lax.all_to_all(part, 'band', 0, 0, tiled=True)  6.33 us
    pallas_call x1, Pallas kernels, local(): pl.pallas_call(denoise_kernel, out_shape=pltpu.VMEM((4, SUB, SPAN), BF16)...  4.05 us
    ppermute x1, starting transfers between devices, local(): before = lax.ppermute(block, 'band', [(b, b + 1) for b in range(bands - 1)])  1.92 us
  transfers between devices with their start and end apart: 7, of which 3 were waited for; matrix products, arithmetic and copies ran while one was open for 1% of the time, Pallas kernels for 2%

profile of v3, /device:TPU:1, one launch (start us, length us, event | category | flops | bytes accessed | tf_op | source)
XLA Modules:
  0.0 70.0 jit_solution(17436202703679009178)
XLA Ops:
  0.6 0.0 copy-start
  0.6 0.0 copy-start.4
  0.7 0.0 copy-start.8
  0.7 0.0 copy-start.9
  0.7 0.0 copy-start.2
  0.7 1.1 %open.1.here_ref = bf16[8,2688]{1,0:T(8,128)(2,1)S(1)} custom-call(f32[1,2,10752]{2,1,0:T(2,128)} %states_ref.3, f32[2,10752]{1,0:T(2,128)} %anchor_ref.3), custom_call_target="tpu_custom_call" | custom-call | flops 10000000000 | bytes 1000000 | tf_op jit(solution)/shard_map/open/pallas_call | solution.py:227
  1.8 0.0 copy-start.1
  1.8 0.0 copy-start.3
  1.8 0.0 copy-start.5
  1.8 8.9 %collective-permute-start.1 = (bf16[8,2688]{1,0:T(8,128)(2,1)S(1)}, bf16[8,2688]{1,0:T(8,128)(2,1)S(1)}, u32[]{:S(2)}, u32[]{:S(2)}) collective-permute-start(bf16[8,2688]{1,0:T(8,128)(2,1)S(1)} %open.1.here_ref), channel_id=1, source_target_pairs={{1,0},{2,1},{3,2},{4,3},{5,4},{6,5},{7,6},{8,7},{9,8},{10,9},{11,1... | collective-permute-start | bytes 129032 | tf_op jit(solution)/shard_map/ppermute | solution.py:236
  10.7 1.9 %collective-permute-start = (bf16[8,2688]{1,0:T(8,128)(2,1)S(1)}, bf16[8,2688]{1,0:T(8,128)(2,1)S(1)}, u32[]{:S(2)}, u32[]{:S(2)}) collective-permute-start(bf16[8,2688]{1,0:T(8,128)(2,1)S(1)} %open.1.here_ref), channel_id=1, source_target_pairs={{0,1},{1,2},{2,3},{3,4},{4,5},{5,6},{6,7},{7,8},{8,9},{9,10},{10,1... | collective-permute-start | bytes 129032 | tf_op jit(solution)/shard_map/ppermute | solution.py:235
  12.6 7.0 %collective-permute-start.2 = (s32[1]{0:T(128)}, s32[1]{0:T(128)}, u32[]{:S(2)}, u32[]{:S(2)}) collective-permute-start(s32[1]{0:T(128)} %param.14), channel_id=1, source_target_pairs={{32,0},{64,32},{96,64},{128,96},{160,128},{192,160},{224,192},{256... | collective-permute-start | bytes 20 | tf_op jit(solution)/shard_map/ppermute | solution.py:234
  19.6 0.8 %collective-permute-done.2 = s32[1]{0:T(128)} collective-permute-done((s32[1]{0:T(128)}, s32[1]{0:T(128)}, u32[]{:S(2)}, u32[]{:S(2)}) %collective-permute-start.2) | collective-permute-done | bytes 36 | tf_op jit(solution)/shard_map/ppermute | solution.py:234
  20.4 0.0 copy-done
  20.4 0.0 copy-done.4
  20.4 0.0 copy-done.8
  20.4 0.0 copy-done.9
  20.4 1.6 %own.1 = (f32[256,512]{1,0:T(8,128)S(1)}, bf16[3,256,512]{2,1,0:T(8,128)(2,1)S(1)}, f32[1,512]{1,0:T(1,128)S(1)}, f32[1,128]{1,0:T(1,128)S(1)}) custom-call(s32[1,1]{1,0:T(1,128)} %bitcast.index_ref, f32[1,20]{1,0:T(1,128)S(1)} %bitcast.10, f32[1,512]{1,0:T(1,128)S(1)} %bitcast.9, bf16[8,2688]{1,0:T(8,128)(2,1)S(1)} %open.1.here_ref, ...), custom_call_target="tpu_custom_call" | custom-call | tf_op jit(solution)/shard_map/own/pallas_call | solution.py:242
  22.0 0.0 collective-permute-done.1.after_ref
  22.0 0.0 collective-permute-done.before_ref
  22.0 0.0 copy-done.2
  22.0 0.0 copy-done.1
  22.0 0.0 copy-done.3
  22.1 0.0 copy-done.5
  22.1 0.0 copy-start.6
  22.1 0.0 copy-start.7
  22.1 0.0 copy-start.10
  22.1 4.1 %denoise.1 = bf16[4,8,2688]{2,1,0:T(8,128)(2,1)S(1)} custom-call(bf16[8,2688]{1,0:T(8,128)(2,1)S(1)} %collective-permute-done.before_ref, bf16[8,2688]{1,0:T(8,128)(2,1)S(1)} %collective-permute-done.1.after_ref, f32[256,512]{1,0:T(8,128)S(1)} %get-tuple-element.11.embedded_ref, bf16[3,256,512]{2,1,0:T(8,128)(2,1)S(1)} %get-tuple-element.12.heads_ref, ...), custom_call_target="tpu_custom_call" | custom-call | tf_op jit(solution)/shard_map/denoise/pallas_call | solution.py:251
  26.2 10.6 %all_to_all.14.group_ref = bf16[4,8,2688]{2,1,0:T(8,128)(2,1)S(1)} all-to-all(bf16[4,8,2688]{2,1,0:T(8,128)(2,1)S(1)} %denoise.1), channel_id=1, replica_groups={{480,0,32,64},{96,128,160,192},{224,256,288,320},{352,384,416,448},{481..., dimensions={0} | all-to-all | bytes 344064 | tf_op jit(solution)/shard_map/all_to_all | solution.py:258
  36.8 5.2 %collective-permute-start.5 = (bf16[8,2688]{1,0:T(8,128)(2,1)S(1)}, bf16[8,2688]{1,0:T(8,128)(2,1)S(1)}, u32[]{:S(2)}, u32[]{:S(2)}) collective-permute-start(bf16[8,2688]{1,0:T(8,128)(2,1)S(1)} %middle.1), channel_id=1, source_target_pairs={{480,352},{0,384},{32,416},{64,448},{96,480},{481,353},{1,385},{33... | collective-permute-start | bytes 129032 | tf_op jit(solution)/shard_map/ppermute | solution.py:269
  42.0 2.3 %collective-permute-start.4 = (bf16[8,2688]{1,0:T(8,128)(2,1)S(1)}, bf16[8,2688]{1,0:T(8,128)(2,1)S(1)}, u32[]{:S(2)}, u32[]{:S(2)}) collective-permute-start(bf16[8,2688]{1,0:T(8,128)(2,1)S(1)} %middle.1), channel_id=1, source_target_pairs={{64,224},{32,256},{0,288},{480,320},{192,352},{160,384},{128,416},... | collective-permute-start | bytes 129032 | tf_op jit(solution)/shard_map/ppermute | solution.py:269
  44.3 5.5 %collective-permute-start.3 = (bf16[8,2688]{1,0:T(8,128)(2,1)S(1)}, bf16[8,2688]{1,0:T(8,128)(2,1)S(1)}, u32[]{:S(2)}, u32[]{:S(2)}) collective-permute-start(bf16[8,2688]{1,0:T(8,128)(2,1)S(1)} %middle.1), channel_id=1, source_target_pairs={{64,96},{0,128},{32,160},{480,192},{96,224},{128,256},{160,288},{1... | collective-permute-start | bytes 129032 | tf_op jit(solution)/shard_map/ppermute | solution.py:269
  49.8 0.0 copy-done.6
  49.8 0.0 copy-done.7
  49.8 0.0 copy-done.10
  49.8 0.2 base.1
  50.0 0.0 collective-permute-done.5.back12_ref
  50.0 0.0 collective-permute-done.4.back8_ref
  50.0 0.9 %collective-permute-done.3.back4_ref = bf16[8,2688]{1,0:T(8,128)(2,1)S(1)} collective-permute-done((bf16[8,2688]{1,0:T(8,128)(2,1)S(1)}, bf16[8,2688]{1,0:T(8,128)(2,1)S(1)}, u32[]{:S(2)}, u32[]{:S(2)}) %collective-permute-start.3) | collective-permute-done | bytes 43040 | tf_op jit(solution)/shard_map/ppermute | solution.py:269
  50.9 0.6 close.1
  51.5 9.1 %all-to-all-start.1 = ((f32[32,1,128]{2,1,0:T(1,128)}), f32[32,1,128]{2,1,0:T(1,128)S(1)}, u32[]{:S(2)}, u32[]{:S(2)}) async-start(f32[32,1,128]{2,1,0:T(1,128)} %bitcast.5), calls=%async_computation.1 | async-start | bytes 32768 | tf_op jit(solution)/shard_map/all_to_all | solution.py:281
  60.6 0.6 copy.15
  61.3 6.3 %all-to-all-done.1 = f32[32,1,128]{2,1,0:T(1,128)S(1)} async-done(((f32[32,1,128]{2,1,0:T(1,128)}), f32[32,1,128]{2,1,0:T(1,128)S(1)}, u32[]{:S(2)}, u32[]{:S(2)}) %all-to-all-start.1) | async-done | bytes 16416 | tf_op jit(solution)/shard_map/all_to_all | solution.py:281
  67.6 0.6 reduce_sum.9
  (1 shorter events, 0.0 us)
Async XLA Ops:
  0.6 19.8 %copy-start = (bf16[512,1536]{1,0:T(8,128)(2,1)S(1)}, bf16[512,1536]{1,0:T(8,128)(2,1)}, u32[]{:S(2)}) copy-start(bf16[512,1536]{1,0:T(8,128)(2,1)} %qkv_ref.3) | copy-start | bytes 4718596
  0.6 19.8 %copy-start.4 = (bf16[84,512]{1,0:T(8,128)(2,1)S(1)}, bf16[84,512]{1,0:T(8,128)(2,1)}, u32[]{:S(2)}) copy-start(bf16[84,512]{1,0:T(8,128)(2,1)} %enc_ref.3) | copy-start | bytes 258052
  0.7 19.8 %copy-start.8 = (f32[512]{0:T(512)S(1)}, f32[512]{0:T(512)}, u32[]{:S(2)}) copy-start(f32[512]{0:T(512)} %param.17) | copy-start | bytes 6148
  0.7 19.8 %copy-start.9 = (f32[20]{0:T(128)S(1)}, f32[20]{0:T(128)}, u32[]{:S(2)}) copy-start(f32[20]{0:T(128)} %param.15) | copy-start | bytes 244
  0.7 21.4 %copy-start.2 = (bf16[1024,512]{1,0:T(8,128)(2,1)S(1)}, bf16[1024,512]{1,0:T(8,128)(2,1)}, u32[]{:S(2)}) copy-start(bf16[1024,512]{1,0:T(8,128)(2,1)} %down_ref.1) | copy-start | bytes 3145732
  1.8 20.3 %copy-start.1 = (bf16[512,1024]{1,0:T(8,128)(2,1)S(1)}, bf16[512,1024]{1,0:T(8,128)(2,1)}, u32[]{:S(2)}) copy-start(bf16[512,1024]{1,0:T(8,128)(2,1)} %up_ref.1) | copy-start | bytes 3145732
  1.8 20.3 %copy-start.3 = (bf16[512,512]{1,0:T(8,128)(2,1)S(1)}, bf16[512,512]{1,0:T(8,128)(2,1)}, u32[]{:S(2)}) copy-start(bf16[512,512]{1,0:T(8,128)(2,1)} %out_w_ref.1) | copy-start | bytes 1572868
  1.8 20.3 %copy-start.5 = (bf16[512,84]{0,1:T(8,128)(2,1)S(1)}, bf16[512,84]{0,1:T(8,128)(2,1)}, u32[]{:S(2)}) copy-start(bf16[512,84]{0,1:T(8,128)(2,1)} %param.22) | copy-start | bytes 258052
  1.8 20.2 %collective-permute-start.1 = (bf16[8,2688]{1,0:T(8,128)(2,1)S(1)}, bf16[8,2688]{1,0:T(8,128)(2,1)S(1)}, u32[]{:S(2)}, u32[]{:S(2)}) collective-permute-start(bf16[8,2688]{1,0:T(8,128)(2,1)S(1)} %open.1.here_ref), channel_id=1, source_target_pairs={{1,0},{2,1},{3,2},{4,3},{5,4},{6,5},{7,6},{8,7},{9,8},{10,9},{11,1... | collective-permute-start | bytes 129032 | tf_op jit(solution)/shard_map/ppermute | solution.py:236
  10.7 11.3 %collective-permute-start = (bf16[8,2688]{1,0:T(8,128)(2,1)S(1)}, bf16[8,2688]{1,0:T(8,128)(2,1)S(1)}, u32[]{:S(2)}, u32[]{:S(2)}) collective-permute-start(bf16[8,2688]{1,0:T(8,128)(2,1)S(1)} %open.1.here_ref), channel_id=1, source_target_pairs={{0,1},{1,2},{2,3},{3,4},{4,5},{5,6},{6,7},{7,8},{8,9},{9,10},{10,1... | collective-permute-start | bytes 129032 | tf_op jit(solution)/shard_map/ppermute | solution.py:235
  12.6 7.8 %collective-permute-start.2 = (s32[1]{0:T(128)}, s32[1]{0:T(128)}, u32[]{:S(2)}, u32[]{:S(2)}) collective-permute-start(s32[1]{0:T(128)} %param.14), channel_id=1, source_target_pairs={{32,0},{64,32},{96,64},{128,96},{160,128},{192,160},{224,192},{256... | collective-permute-start | bytes 20 | tf_op jit(solution)/shard_map/ppermute | solution.py:234
  22.1 27.7 %copy-start.6 = (f32[1,2,10752]{2,1,0:T(2,128)S(1)}, f32[1,2,10752]{2,1,0:T(2,128)}, u32[]{:S(2)}) copy-start(f32[1,2,10752]{2,1,0:T(2,128)} %states_ref.3) | copy-start | bytes 258052
  22.1 27.7 %copy-start.7 = (f32[2,10752]{1,0:T(2,128)S(1)}, f32[2,10752]{1,0:T(2,128)}, u32[]{:S(2)}) copy-start(f32[2,10752]{1,0:T(2,128)} %anchor_ref.3) | copy-start | bytes 258052
  22.1 27.7 %copy-start.10 = (f32[1,64]{1,0:T(1,128)S(1)}, f32[1,64]{1,0:T(1,128)}, u32[]{:S(2)}) copy-start(f32[1,64]{1,0:T(1,128)} %constant.12.area_ref) | copy-start | bytes 772
  36.8 13.2 %collective-permute-start.5 = (bf16[8,2688]{1,0:T(8,128)(2,1)S(1)}, bf16[8,2688]{1,0:T(8,128)(2,1)S(1)}, u32[]{:S(2)}, u32[]{:S(2)}) collective-permute-start(bf16[8,2688]{1,0:T(8,128)(2,1)S(1)} %middle.1), channel_id=1, source_target_pairs={{480,352},{0,384},{32,416},{64,448},{96,480},{481,353},{1,385},{33... | collective-permute-start | bytes 129032 | tf_op jit(solution)/shard_map/ppermute | solution.py:269
  42.0 8.0 %collective-permute-start.4 = (bf16[8,2688]{1,0:T(8,128)(2,1)S(1)}, bf16[8,2688]{1,0:T(8,128)(2,1)S(1)}, u32[]{:S(2)}, u32[]{:S(2)}) collective-permute-start(bf16[8,2688]{1,0:T(8,128)(2,1)S(1)} %middle.1), channel_id=1, source_target_pairs={{64,224},{32,256},{0,288},{480,320},{192,352},{160,384},{128,416},... | collective-permute-start | bytes 129032 | tf_op jit(solution)/shard_map/ppermute | solution.py:269
  44.3 6.6 %collective-permute-start.3 = (bf16[8,2688]{1,0:T(8,128)(2,1)S(1)}, bf16[8,2688]{1,0:T(8,128)(2,1)S(1)}, u32[]{:S(2)}, u32[]{:S(2)}) collective-permute-start(bf16[8,2688]{1,0:T(8,128)(2,1)S(1)} %middle.1), channel_id=1, source_target_pairs={{64,96},{0,128},{32,160},{480,192},{96,224},{128,256},{160,288},{1... | collective-permute-start | bytes 129032 | tf_op jit(solution)/shard_map/ppermute | solution.py:269
  51.5 16.1 %all-to-all-start.1 = ((f32[32,1,128]{2,1,0:T(1,128)}), f32[32,1,128]{2,1,0:T(1,128)S(1)}, u32[]{:S(2)}, u32[]{:S(2)}) async-start(f32[32,1,128]{2,1,0:T(1,128)} %bitcast.5), calls=%async_computation.1 | async-start | bytes 32768 | tf_op jit(solution)/shard_map/all_to_all | solution.py:281

commit v4 on v3

--- a/solution.py
+++ b/solution.py
@@ -48,18 +48,26 @@
     return jnp.concatenate([rows[:, g * SPAN : (g + 1) * SPAN] for g in range(PACKS)], axis=0)
 
 
-def open_kernel(states_ref, anchor_ref, out_ref, rows_ref):
+def sight_kernel(sight_ref):
+    band = lax.axis_index("band")
+    q_row = lax.broadcasted_iota(jnp.int32, (TOK, TOK), 0) % 2
+    k_row = lax.broadcasted_iota(jnp.int32, (TOK, TOK), 1) % 2
+    before = ((q_row == 0) | (k_row == 1)) & (band > 0)
+    after = ((q_row == 1) | (k_row == 0)) & (band < lax.axis_size("band") - 1)
+    sight_ref[0] = before.astype(F32)
+    sight_ref[1] = after.astype(F32)
+
+
+def open_kernel(states_ref, anchor_ref, sight_ref, out_ref):
     last = lax.axis_index("step") == lax.axis_size("step") - 1
 
     @pl.when(last)
     def _():
-        pltpu.sync_copy(anchor_ref, rows_ref)
+        out_ref[...] = to_packed(anchor_ref[...]).astype(BF16)
 
     @pl.when(jnp.logical_not(last))
     def _():
-        pltpu.sync_copy(states_ref.at[0], rows_ref)
-
-    out_ref[...] = to_packed(rows_ref[...]).astype(BF16)
+        out_ref[...] = to_packed(states_ref[0]).astype(BF16)
 
 
 def unpack_tokens(block_ref, tok_ref):
@@ -90,9 +98,19 @@
     ).astype(BF16)
 
 
+def attend(queries, keys, values, mask):
+    scores = lax.dot_general(
+        queries, keys, (((1,), (1,)), ((), ())), preferred_element_type=F32
+    )
+    weights = jnp.exp(scores * SCORE)
+    if mask is not None:
+        weights = weights * mask
+    return jnp.sum(weights, axis=-1, keepdims=True), mm(weights.astype(BF16), values)
+
+
 def own_kernel(
-    index_ref, sigma_ref, embed_ref, here_ref, enc_ref, qkv_ref, embedded_ref, heads_ref,
-    offset_ref, noise_ref, tok_ref,
+    index_ref, sigma_ref, embed_ref, here_ref, enc_ref, qkv_ref, embedded_ref, queries_ref,
+    total_ref, mix_ref, offset_ref, noise_ref, tok_ref,
 ):
     level = lax.broadcasted_iota(jnp.int32, (1, LEVELS), 1)
     noise = jnp.sum(
@@ -103,43 +121,32 @@
     noise_ref[...] = jnp.broadcast_to(noise, noise_ref.shape)
     embedded, normed = embed(here_ref, tok_ref, enc_ref, offset)
     embedded_ref[...] = embedded
-    heads_ref[0] = heads_of(mm(normed, qkv_ref[:, :W]))
-    heads_ref[1] = heads_of(mm(normed, qkv_ref[:, W : 2 * W]))
-    heads_ref[2] = mm(normed, qkv_ref[:, 2 * W :]).astype(BF16)
+    queries = heads_of(mm(normed, qkv_ref[:, :W]))
+    queries_ref[...] = queries
+    keys = heads_of(mm(normed, qkv_ref[:, W : 2 * W]))
+    values = mm(normed, qkv_ref[:, 2 * W :]).astype(BF16)
+    for h in range(HEADS):
+        at = slice(h * HEAD_DIM, (h + 1) * HEAD_DIM)
+        total_ref[h], mix_ref[h] = attend(queries[:, at], keys[:, at], values[:, at], None)
 
 
 def denoise_kernel(
-    before_ref, after_ref, embedded_ref, heads_ref, offset_ref, noise_ref, enc_ref, qkv_ref,
-    out_w_ref, up_ref, down_ref, dec_ref, copies_ref, tok_ref,
+    before_ref, after_ref, embedded_ref, queries_ref, total_ref, mix_ref, offset_ref, noise_ref,
+    sight_ref, enc_ref, qkv_ref, out_w_ref, up_ref, down_ref, dec_ref, copies_ref, tok_ref,
 ):
-    band = lax.axis_index("band")
-    bands = lax.axis_size("band")
     offset = offset_ref[...]
     blocks = [embed(ref, tok_ref, enc_ref, offset)[1] for ref in (before_ref, after_ref)]
-    queries = heads_ref[0]
-    keys = [heads_ref[1]] + [heads_of(mm(n, qkv_ref[:, W : 2 * W])) for n in blocks]
-    values = [heads_ref[2]] + [mm(n, qkv_ref[:, 2 * W :]).astype(BF16) for n in blocks]
-
-    q_row = lax.broadcasted_iota(jnp.int32, (TOK, TOK), 0) % 2
-    k_row = lax.broadcasted_iota(jnp.int32, (TOK, TOK), 1) % 2
-    see_before = (((q_row == 0) | (k_row == 1)) & (band > 0)).astype(F32)
-    see_after = (((q_row == 1) | (k_row == 0)) & (band < bands - 1)).astype(F32)
-    masks = [None, see_before, see_after]
+    queries = queries_ref[...]
+    keys = [heads_of(mm(n, qkv_ref[:, W : 2 * W])) for n in blocks]
+    values = [mm(n, qkv_ref[:, 2 * W :]).astype(BF16) for n in blocks]
 
     attended = []
     for h in range(HEADS):
         at = slice(h * HEAD_DIM, (h + 1) * HEAD_DIM)
-        total, mix = 0.0, 0.0
-        for n in range(3):
-            scores = lax.dot_general(
-                queries[:, at], keys[n][:, at], (((1,), (1,)), ((), ())),
-                preferred_element_type=F32,
-            )
-            weights = jnp.exp(scores * SCORE)
-            if masks[n] is not None:
-                weights = weights * masks[n]
-            total = total + jnp.sum(weights, axis=-1, keepdims=True)
-            mix = mix + mm(weights.astype(BF16), values[n][:, at])
+        total, mix = total_ref[h], mix_ref[h]
+        for n in range(2):
+            more, part = attend(queries[:, at], keys[n][:, at], values[n][:, at], sight_ref[n])
+            total, mix = total + more, mix + part
         attended.append((mix / total).astype(BF16))
     attended = jnp.concatenate(attended, axis=1)
 
@@ -212,10 +219,6 @@
     return [pltpu.with_memory_space_constraint(a, pltpu.VMEM) for a in arrays]
 
 
-def in_hbm(*arrays):
-    return [pltpu.with_memory_space_constraint(a, pltpu.HBM) for a in arrays]
-
-
 def local(
     states, anchor, step_index, sigmas, enc_w, noise_embed, qkv_w, out_w, up_w, down_w, dec_w
 ):
@@ -224,12 +227,16 @@
     smem = pl.BlockSpec(memory_space=pltpu.SMEM)
     hbm = pl.BlockSpec(memory_space=pltpu.HBM)
 
+    sight = pl.pallas_call(
+        sight_kernel, out_shape=pltpu.VMEM((2, TOK, TOK), F32), out_specs=vmem, name="sight",
+        cost_estimate=pl.CostEstimate(flops=10**10, bytes_accessed=10**6, transcendentals=0),
+        compiler_params=pltpu.CompilerParams(vmem_limit_bytes=8 << 20),
+    )()
     block = pl.pallas_call(
-        open_kernel, out_shape=pltpu.VMEM((SUB, SPAN), BF16), in_specs=[hbm] * 2, out_specs=vmem,
-        scratch_shapes=[pltpu.VMEM((2, LON * C), F32)],
+        open_kernel, out_shape=pltpu.VMEM((SUB, SPAN), BF16), in_specs=[vmem] * 3, out_specs=vmem,
         cost_estimate=pl.CostEstimate(flops=10**10, bytes_accessed=10**6, transcendentals=0),
         name="open", compiler_params=pltpu.CompilerParams(vmem_limit_bytes=8 << 20),
-    )(*in_hbm(states, anchor))
+    )(*local_vmem(states, anchor, sight))
 
     index = lax.ppermute(step_index, "step", [((s + 1) % steps, s) for s in range(steps)])
     before = lax.ppermute(block, "band", [(b, b + 1) for b in range(bands - 1)])
@@ -242,18 +249,19 @@
     own = pl.pallas_call(
         own_kernel,
         out_shape=(
-            pltpu.VMEM((TOK, W), F32), pltpu.VMEM((3, TOK, W), BF16), pltpu.VMEM((1, W), F32),
-            pltpu.VMEM((1, LANES), F32),
+            pltpu.VMEM((TOK, W), F32), pltpu.VMEM((TOK, W), BF16),
+            pltpu.VMEM((HEADS, TOK, 1), F32), pltpu.VMEM((HEADS, TOK, HEAD_DIM), F32),
+            pltpu.VMEM((1, W), F32), pltpu.VMEM((1, LANES), F32),
         ),
-        in_specs=[vmem] * 6, out_specs=(vmem,) * 4, scratch_shapes=[tokens],
+        in_specs=[vmem] * 6, out_specs=(vmem,) * 6, scratch_shapes=[tokens],
         name="own", compiler_params=limit(16),
     )(*local_vmem(index[None], sigmas[None], noise_embed[None], block, enc_w, qkv_w))
     copies = pl.pallas_call(
         denoise_kernel,
         out_shape=pltpu.VMEM((4, SUB, SPAN), BF16),
-        in_specs=[vmem] * 12, out_specs=vmem, scratch_shapes=[tokens],
+        in_specs=[vmem] * 15, out_specs=vmem, scratch_shapes=[tokens],
         name="denoise", compiler_params=limit(32),
-    )(*local_vmem(before, after, *own, enc_w, qkv_w, out_w, up_w, down_w, dec_w.T))
+    )(*local_vmem(before, after, *own, sight, enc_w, qkv_w, out_w, up_w, down_w, dec_w.T))
 
     group = lax.all_to_all(
         copies, "step", 0, 0, tiled=True,

time: 70.8 us -> 70.9 us (level)
  local copies, waits for them, and re-layouts: 0.7 us -> 1.52 us
  Pallas kernels: 7.55 us -> 6.74 us
    pallas_call x1, Pallas kernels: 1.08 us -> 0.04 us  [local(): pl.pallas_call(open_kernel, out_shape=pltpu.VMEM((SUB, SPAN), BF16), in_s...]
    unnamed x23, local copies, waits for them, and re-layouts: 0.7 us -> 1.52 us
  transfers between devices with their start and end apart: 7 -> 7, of which waited for: 3 -> 3; matrix products, arithmetic and copies ran while one was open for 1% -> 1% of each run, Pallas kernels for 2% -> 3%
where the time goes in v4:
time: 70.9 us; the launch traced here: 70.1 us
  starting transfers between devices  39.9 us (56%)
  blocking collectives  10.6 us (15%)
  waiting for transfers between devices  8.09 us (11%)
  Pallas kernels  6.74 us (10%)
  between operations  2.62 us (4%)
  local copies, waits for them, and re-layouts  1.52 us (2%)
    ppermute x3, starting transfers between devices, local(): far.append(lax.ppermute(sent, 'step', pairs))  12.9 us
    all_to_all x1, blocking collectives, local(): lax.all_to_all(copies, 'step', 0, 0, tiled=True, axis_index_groups=[[(4 *...  10.6 us
    all_to_all x1, starting transfers between devices, local(): parts = lax.all_to_all(part, 'band', 0, 0, tiled=True)  9.09 us
    ppermute x1, starting transfers between devices, local(): after = lax.ppermute(block, 'band', [(b + 1, b) for b in range(bands - 1)])  9.01 us
    ppermute x1, starting transfers between devices, local(): lax.ppermute(step_index, 'step', [((s + 1) % steps, s) for s in range(ste...  6.96 us
    all_to_all x1, waiting for transfers between devices, local(): parts = lax.all_to_all(part, 'band', 0, 0, tiled=True)  6.33 us
    pallas_call x1, Pallas kernels, local(): pl.pallas_call(denoise_kernel, out_shape=pltpu.VMEM((4, SUB, SPAN), BF16)...  3.75 us
    pallas_call x1, Pallas kernels, local(): pl.pallas_call(own_kernel, out_shape=(pltpu.VMEM((TOK, W), F32), pltpu.VM...  2.03 us
  transfers between devices with their start and end apart: 7, of which 3 were waited for; matrix products, arithmetic and copies ran while one was open for 1% of the time, Pallas kernels for 3%

profile of v4, /device:TPU:1, one launch (start us, length us, event | category | flops | bytes accessed | tf_op | source)
XLA Modules:
  0.0 70.1 jit_solution(936350987022599818)
XLA Ops:
  0.6 0.0 copy-start.7
  0.6 0.0 copy-start.6
  0.6 0.1 sight.1.sight_ref
  0.7 0.8 %copy-done.7 = f32[2,10752]{1,0:T(2,128)S(1)} copy-done((f32[2,10752]{1,0:T(2,128)S(1)}, f32[2,10752]{1,0:T(2,128)}, u32[]{:S(2)}) %copy-start.7) | copy-done | bytes 86040
  1.5 0.0 copy-done.6
  1.6 0.0 copy-start
  1.6 0.0 copy-start.4
  1.6 0.0 copy-start.8
  1.6 0.0 copy-start.9
  1.6 0.0 copy-start.2
  1.6 0.0 copy-start.1
  1.6 0.0 copy-start.3
  1.7 0.0 copy-start.5
  1.7 9.0 %collective-permute-start.1 = (bf16[8,2688]{1,0:T(8,128)(2,1)S(1)}, bf16[8,2688]{1,0:T(8,128)(2,1)S(1)}, u32[]{:S(2)}, u32[]{:S(2)}) collective-permute-start(bf16[8,2688]{1,0:T(8,128)(2,1)S(1)} %open.1.here_ref), channel_id=1, source_target_pairs={{1,0},{2,1},{3,2},{4,3},{5,4},{6,5},{7,6},{8,7},{9,8},{10,9},{11,1... | collective-permute-start | bytes 129032 | tf_op jit(solution)/shard_map/ppermute | solution.py:243
  10.7 1.9 %collective-permute-start = (bf16[8,2688]{1,0:T(8,128)(2,1)S(1)}, bf16[8,2688]{1,0:T(8,128)(2,1)S(1)}, u32[]{:S(2)}, u32[]{:S(2)}) collective-permute-start(bf16[8,2688]{1,0:T(8,128)(2,1)S(1)} %open.1.here_ref), channel_id=1, source_target_pairs={{0,1},{1,2},{2,3},{3,4},{4,5},{5,6},{6,7},{7,8},{8,9},{9,10},{10,1... | collective-permute-start | bytes 129032 | tf_op jit(solution)/shard_map/ppermute | solution.py:242
  12.6 7.0 %collective-permute-start.2 = (s32[1]{0:T(128)}, s32[1]{0:T(128)}, u32[]{:S(2)}, u32[]{:S(2)}) collective-permute-start(s32[1]{0:T(128)} %param.14), channel_id=1, source_target_pairs={{32,0},{64,32},{96,64},{128,96},{160,128},{192,160},{224,192},{256... | collective-permute-start | bytes 20 | tf_op jit(solution)/shard_map/ppermute | solution.py:241
  19.6 0.8 %collective-permute-done.2 = s32[1]{0:T(128)} collective-permute-done((s32[1]{0:T(128)}, s32[1]{0:T(128)}, u32[]{:S(2)}, u32[]{:S(2)}) %collective-permute-start.2) | collective-permute-done | bytes 36 | tf_op jit(solution)/shard_map/ppermute | solution.py:241
  20.4 0.0 copy-done
  20.4 0.0 copy-done.4
  20.4 0.0 copy-done.8
  20.4 0.0 copy-done.9
  20.4 2.0 %own.1 = (f32[256,512]{1,0:T(8,128)S(1)}, bf16[256,512]{1,0:T(8,128)(2,1)S(1)}, f32[4,256,1]{2,1,0:T(8,128)S(1)}, f32[4,256,128]{2,1,0:T(8,128)S(1)}, f32[1,512]{1,0:T(1,128)S(1)}, /*index=5*/f32[1,128]{1,0:T(1,128)S(1)}) custom-call(s32[1,1]{1,0:T(1,128)} %bitcast.index_ref, f32[1,20]{1,0:T(1,128)S(1)} %bitcast.10, f32[1,512]{1,0:T(1,128)S(1)} %bitcast.9, ...), custom_call_target="tpu_custom_call" | custom-call | tf_op jit(solution)/shard_map/own/pallas_call | solution.py:249
  22.5 0.0 collective-permute-done.1.after_ref
  22.5 0.0 collective-permute-done.before_ref
  22.5 0.0 copy-done.2
  22.5 0.0 copy-done.1
  22.5 0.0 copy-done.3
  22.5 0.0 copy-done.5
  22.5 0.0 copy-start.10
  22.5 3.7 %denoise.1 = bf16[4,8,2688]{2,1,0:T(8,128)(2,1)S(1)} custom-call(bf16[8,2688]{1,0:T(8,128)(2,1)S(1)} %collective-permute-done.before_ref, bf16[8,2688]{1,0:T(8,128)(2,1)S(1)} %collective-permute-done.1.after_ref, f32[256,512]{1,0:T(8,128)S(1)} %get-tuple-element.13.embedded_ref, bf16[256,512]{1,0:T(8,128)(2,1)S(1)} %get-tuple-element.14.queries_ref, ...), custom_call_target="tpu_custom_call" | custom-call | tf_op jit(solution)/shard_map/denoise/pallas_call | solution.py:259
  26.3 10.6 %all_to_all.14.group_ref = bf16[4,8,2688]{2,1,0:T(8,128)(2,1)S(1)} all-to-all(bf16[4,8,2688]{2,1,0:T(8,128)(2,1)S(1)} %denoise.1), channel_id=1, replica_groups={{480,0,32,64},{96,128,160,192},{224,256,288,320},{352,384,416,448},{481..., dimensions={0} | all-to-all | bytes 344064 | tf_op jit(solution)/shard_map/all_to_all | solution.py:266
  36.9 5.2 %collective-permute-start.5 = (bf16[8,2688]{1,0:T(8,128)(2,1)S(1)}, bf16[8,2688]{1,0:T(8,128)(2,1)S(1)}, u32[]{:S(2)}, u32[]{:S(2)}) collective-permute-start(bf16[8,2688]{1,0:T(8,128)(2,1)S(1)} %middle.1), channel_id=1, source_target_pairs={{480,352},{0,384},{32,416},{64,448},{96,480},{481,353},{1,385},{33... | collective-permute-start | bytes 129032 | tf_op jit(solution)/shard_map/ppermute | solution.py:277
  42.1 2.3 %collective-permute-start.4 = (bf16[8,2688]{1,0:T(8,128)(2,1)S(1)}, bf16[8,2688]{1,0:T(8,128)(2,1)S(1)}, u32[]{:S(2)}, u32[]{:S(2)}) collective-permute-start(bf16[8,2688]{1,0:T(8,128)(2,1)S(1)} %middle.1), channel_id=1, source_target_pairs={{64,224},{32,256},{0,288},{480,320},{192,352},{160,384},{128,416},... | collective-permute-start | bytes 129032 | tf_op jit(solution)/shard_map/ppermute | solution.py:277
  44.4 5.5 %collective-permute-start.3 = (bf16[8,2688]{1,0:T(8,128)(2,1)S(1)}, bf16[8,2688]{1,0:T(8,128)(2,1)S(1)}, u32[]{:S(2)}, u32[]{:S(2)}) collective-permute-start(bf16[8,2688]{1,0:T(8,128)(2,1)S(1)} %middle.1), channel_id=1, source_target_pairs={{64,96},{0,128},{32,160},{480,192},{96,224},{128,256},{160,288},{1... | collective-permute-start | bytes 129032 | tf_op jit(solution)/shard_map/ppermute | solution.py:277
  49.9 0.0 copy-done.10
  49.9 0.2 base.1
  50.1 0.0 collective-permute-done.5.back12_ref
  50.1 0.0 collective-permute-done.4.back8_ref
  50.1 0.9 %collective-permute-done.3.back4_ref = bf16[8,2688]{1,0:T(8,128)(2,1)S(1)} collective-permute-done((bf16[8,2688]{1,0:T(8,128)(2,1)S(1)}, bf16[8,2688]{1,0:T(8,128)(2,1)S(1)}, u32[]{:S(2)}, u32[]{:S(2)}) %collective-permute-start.3) | collective-permute-done | bytes 43040 | tf_op jit(solution)/shard_map/ppermute | solution.py:277
  51.0 0.6 close.1
  51.7 9.1 %all-to-all-start.1 = ((f32[32,1,128]{2,1,0:T(1,128)}), f32[32,1,128]{2,1,0:T(1,128)S(1)}, u32[]{:S(2)}, u32[]{:S(2)}) async-start(f32[32,1,128]{2,1,0:T(1,128)} %bitcast.5), calls=%async_computation.1 | async-start | bytes 32768 | tf_op jit(solution)/shard_map/all_to_all | solution.py:289
  60.8 0.6 copy.15
  61.4 6.3 %all-to-all-done.1 = f32[32,1,128]{2,1,0:T(1,128)S(1)} async-done(((f32[32,1,128]{2,1,0:T(1,128)}), f32[32,1,128]{2,1,0:T(1,128)S(1)}, u32[]{:S(2)}, u32[]{:S(2)}) %all-to-all-start.1) | async-done | bytes 16416 | tf_op jit(solution)/shard_map/all_to_all | solution.py:289
  67.7 0.6 reduce_sum.9
  (2 shorter events, 0.1 us)
Async XLA Ops:
  0.6 0.9 %copy-start.7 = (f32[2,10752]{1,0:T(2,128)S(1)}, f32[2,10752]{1,0:T(2,128)}, u32[]{:S(2)}) copy-start(f32[2,10752]{1,0:T(2,128)} %anchor_ref.3) | copy-start | bytes 258052
  0.6 0.9 %copy-start.6 = (f32[1,2,10752]{2,1,0:T(2,128)S(1)}, f32[1,2,10752]{2,1,0:T(2,128)}, u32[]{:S(2)}) copy-start(f32[1,2,10752]{2,1,0:T(2,128)} %states_ref.3) | copy-start | bytes 258052
  1.6 18.9 %copy-start = (bf16[512,1536]{1,0:T(8,128)(2,1)S(1)}, bf16[512,1536]{1,0:T(8,128)(2,1)}, u32[]{:S(2)}) copy-start(bf16[512,1536]{1,0:T(8,128)(2,1)} %qkv_ref.3) | copy-start | bytes 4718596
  1.6 18.9 %copy-start.4 = (bf16[84,512]{1,0:T(8,128)(2,1)S(1)}, bf16[84,512]{1,0:T(8,128)(2,1)}, u32[]{:S(2)}) copy-start(bf16[84,512]{1,0:T(8,128)(2,1)} %enc_ref.3) | copy-start | bytes 258052
  1.6 18.9 %copy-start.8 = (f32[512]{0:T(512)S(1)}, f32[512]{0:T(512)}, u32[]{:S(2)}) copy-start(f32[512]{0:T(512)} %param.17) | copy-start | bytes 6148
  1.6 18.9 %copy-start.9 = (f32[20]{0:T(128)S(1)}, f32[20]{0:T(128)}, u32[]{:S(2)}) copy-start(f32[20]{0:T(128)} %param.15) | copy-start | bytes 244
  1.6 20.9 %copy-start.2 = (bf16[1024,512]{1,0:T(8,128)(2,1)S(1)}, bf16[1024,512]{1,0:T(8,128)(2,1)}, u32[]{:S(2)}) copy-start(bf16[1024,512]{1,0:T(8,128)(2,1)} %down_ref.1) | copy-start | bytes 3145732
  1.6 20.9 %copy-start.1 = (bf16[512,1024]{1,0:T(8,128)(2,1)S(1)}, bf16[512,1024]{1,0:T(8,128)(2,1)}, u32[]{:S(2)}) copy-start(bf16[512,1024]{1,0:T(8,128)(2,1)} %up_ref.1) | copy-start | bytes 3145732
  1.6 20.9 %copy-start.3 = (bf16[512,512]{1,0:T(8,128)(2,1)S(1)}, bf16[512,512]{1,0:T(8,128)(2,1)}, u32[]{:S(2)}) copy-start(bf16[512,512]{1,0:T(8,128)(2,1)} %out_w_ref.1) | copy-start | bytes 1572868
  1.7 20.9 %copy-start.5 = (bf16[512,84]{0,1:T(8,128)(2,1)S(1)}, bf16[512,84]{0,1:T(8,128)(2,1)}, u32[]{:S(2)}) copy-start(bf16[512,84]{0,1:T(8,128)(2,1)} %param.22) | copy-start | bytes 258052
  1.7 20.8 %collective-permute-start.1 = (bf16[8,2688]{1,0:T(8,128)(2,1)S(1)}, bf16[8,2688]{1,0:T(8,128)(2,1)S(1)}, u32[]{:S(2)}, u32[]{:S(2)}) collective-permute-start(bf16[8,2688]{1,0:T(8,128)(2,1)S(1)} %open.1.here_ref), channel_id=1, source_target_pairs={{1,0},{2,1},{3,2},{4,3},{5,4},{6,5},{7,6},{8,7},{9,8},{10,9},{11,1... | collective-permute-start | bytes 129032 | tf_op jit(solution)/shard_map/ppermute | solution.py:243
  10.7 11.8 %collective-permute-start = (bf16[8,2688]{1,0:T(8,128)(2,1)S(1)}, bf16[8,2688]{1,0:T(8,128)(2,1)S(1)}, u32[]{:S(2)}, u32[]{:S(2)}) collective-permute-start(bf16[8,2688]{1,0:T(8,128)(2,1)S(1)} %open.1.here_ref), channel_id=1, source_target_pairs={{0,1},{1,2},{2,3},{3,4},{4,5},{5,6},{6,7},{7,8},{8,9},{9,10},{10,1... | collective-permute-start | bytes 129032 | tf_op jit(solution)/shard_map/ppermute | solution.py:242
  12.6 7.8 %collective-permute-start.2 = (s32[1]{0:T(128)}, s32[1]{0:T(128)}, u32[]{:S(2)}, u32[]{:S(2)}) collective-permute-start(s32[1]{0:T(128)} %param.14), channel_id=1, source_target_pairs={{32,0},{64,32},{96,64},{128,96},{160,128},{192,160},{224,192},{256... | collective-permute-start | bytes 20 | tf_op jit(solution)/shard_map/ppermute | solution.py:241
  22.5 27.4 %copy-start.10 = (f32[1,64]{1,0:T(1,128)S(1)}, f32[1,64]{1,0:T(1,128)}, u32[]{:S(2)}) copy-start(f32[1,64]{1,0:T(1,128)} %constant.12.area_ref) | copy-start | bytes 772
  36.9 13.2 %collective-permute-start.5 = (bf16[8,2688]{1,0:T(8,128)(2,1)S(1)}, bf16[8,2688]{1,0:T(8,128)(2,1)S(1)}, u32[]{:S(2)}, u32[]{:S(2)}) collective-permute-start(bf16[8,2688]{1,0:T(8,128)(2,1)S(1)} %middle.1), channel_id=1, source_target_pairs={{480,352},{0,384},{32,416},{64,448},{96,480},{481,353},{1,385},{33... | collective-permute-start | bytes 129032 | tf_op jit(solution)/shard_map/ppermute | solution.py:277
  42.1 8.0 %collective-permute-start.4 = (bf16[8,2688]{1,0:T(8,128)(2,1)S(1)}, bf16[8,2688]{1,0:T(8,128)(2,1)S(1)}, u32[]{:S(2)}, u32[]{:S(2)}) collective-permute-start(bf16[8,2688]{1,0:T(8,128)(2,1)S(1)} %middle.1), channel_id=1, source_target_pairs={{64,224},{32,256},{0,288},{480,320},{192,352},{160,384},{128,416},... | collective-permute-start | bytes 129032 | tf_op jit(solution)/shard_map/ppermute | solution.py:277
  44.4 6.6 %collective-permute-start.3 = (bf16[8,2688]{1,0:T(8,128)(2,1)S(1)}, bf16[8,2688]{1,0:T(8,128)(2,1)S(1)}, u32[]{:S(2)}, u32[]{:S(2)}) collective-permute-start(bf16[8,2688]{1,0:T(8,128)(2,1)S(1)} %middle.1), channel_id=1, source_target_pairs={{64,96},{0,128},{32,160},{480,192},{96,224},{128,256},{160,288},{1... | collective-permute-start | bytes 129032 | tf_op jit(solution)/shard_map/ppermute | solution.py:277
  51.7 16.1 %all-to-all-start.1 = ((f32[32,1,128]{2,1,0:T(1,128)}), f32[32,1,128]{2,1,0:T(1,128)S(1)}, u32[]{:S(2)}, u32[]{:S(2)}) async-start(f32[32,1,128]{2,1,0:T(1,128)} %bitcast.5), calls=%async_computation.1 | async-start | bytes 32768 | tf_op jit(solution)/shard_map/all_to_all | solution.py:289

commit v5 on v4

--- a/solution.py
+++ b/solution.py
@@ -23,11 +23,10 @@
 TILES = SPAN // LANES
 TOK = 2 * LON
 
-FAR = (
-    [(2, 3), (0, 4), (1, 5), (15, 6)] + [(s, s + 4) for s in range(3, 11)] + [(14, 15)],
-    [(2, 7), (1, 8), (0, 9), (15, 10), (6, 11), (5, 12), (4, 13), (3, 14), (10, 15)],
-    [(15, 11), (0, 12), (1, 13), (2, 14), (3, 15)],
-)
+NEAR = [(15, 3)] + [(s, s + 4) for s in range(7)]
+SKIP = [(2, 7), (1, 8), (0, 9), (15, 10), (14, 15)]
+NEXT = [(s, s + 4) for s in range(7, 11)]
+PAIR = [(6, 11), (5, 12), (4, 13), (3, 14), (10, 15)]
 
 epsilon = 1e-06
 SCORE = 3.0 / math.sqrt(HEAD_DIM)
@@ -182,6 +181,10 @@
     sent_ref[...] = ((parts[0] + parts[1]) + (parts[2] + parts[3])).astype(BF16)
 
 
+def both_kernel(sent_ref, near_ref, both_ref):
+    both_ref[...] = (sent_ref[...].astype(F32) + near_ref[...].astype(F32)).astype(BF16)
+
+
 def base_kernel(group_ref, anchor_ref, states_ref, area_ref, base_ref, old_ref, scale_ref):
     step = lax.axis_index("step")
     band = lax.axis_index("band")
@@ -199,10 +202,11 @@
 
 
 def close_kernel(
-    back4_ref, back8_ref, back12_ref, base_ref, old_ref, scale_ref, new_ref, part_ref
+    near_ref, skip_ref, next_ref, pair_ref, base_ref, old_ref, scale_ref, new_ref, part_ref
 ):
     new = base_ref[...] + (
-        back4_ref[...].astype(F32) + back8_ref[...].astype(F32) + back12_ref[...].astype(F32)
+        (near_ref[...].astype(F32) + next_ref[...].astype(F32))
+        + (skip_ref[...].astype(F32) + pair_ref[...].astype(F32))
     )
     for g in range(PACKS):
         new_ref[0, :, g * SPAN : (g + 1) * SPAN] = new[2 * g : 2 * g + 2, :]
@@ -272,9 +276,19 @@
         middle_kernel, out_shape=pltpu.VMEM((SUB, SPAN), BF16), in_specs=[vmem], out_specs=vmem,
         name="middle", compiler_params=limit(8),
     )(*local_vmem(group))
-    far = []
-    for pairs in FAR:
-        far.append(lax.ppermute(sent, "step", pairs))
+
+    def moved(array, pairs):
+        return lax.ppermute(array, "step", pairs)
+
+    near = moved(sent, NEAR)
+    skip = moved(sent, SKIP)
+    following = moved(sent, NEXT)
+    both = pl.pallas_call(
+        both_kernel, out_shape=pltpu.VMEM((SUB, SPAN), BF16), in_specs=[vmem] * 2, out_specs=vmem,
+        name="both", compiler_params=limit(8),
+    )(*local_vmem(sent, near))
+    pair = moved(both, PAIR)
+    far = (near, skip, following, pair)
     latitude = np.pi * ((np.arange(NLAT, dtype=np.float32) + 0.5) / NLAT - 0.5)
     area = np.cos(latitude).astype(np.float32)
     base = pl.pallas_call(
@@ -284,7 +298,7 @@
     new_states, part = pl.pallas_call(
         close_kernel,
         out_shape=(pltpu.VMEM(states.shape, F32), pltpu.VMEM((bands, LANES), F32)),
-        in_specs=[vmem] * 6, out_specs=(vmem, vmem), name="close", compiler_params=limit(8),
+        in_specs=[vmem] * 7, out_specs=(vmem, vmem), name="close", compiler_params=limit(8),
     )(*local_vmem(*far, *base))
     parts = lax.all_to_all(part, "band", 0, 0, tiled=True)
     change = jnp.sum(parts)[None] / (np.float32(area.sum()) * (LON * C))

time: 70.9 us -> 70.2 us (level)
    ppermute x3 -> x4, starting transfers between devices: 12.9 us -> 13.3 us  [moved(): return lax.ppermute(array, 'step', pairs)]
  transfers between devices with their start and end apart: 7 -> 8, of which waited for: 3 -> 3; matrix products, arithmetic and copies ran while one was open for 1% -> 1% of each run, Pallas kernels for 3% -> 3%
where the time goes in v5:
time: 70.2 us; the launch traced here: 69.9 us
  starting transfers between devices  40.3 us (57%)
  blocking collectives  10.2 us (15%)
  waiting for transfers between devices  7.95 us (11%)
  Pallas kernels  6.63 us (9%)
  between operations  2.64 us (4%)
  local copies, waits for them, and re-layouts  1.52 us (2%)
    ppermute x4, starting transfers between devices, moved(): return lax.ppermute(array, 'step', pairs)  13.3 us
    all_to_all x1, blocking collectives, local(): lax.all_to_all(copies, 'step', 0, 0, tiled=True, axis_index_groups=[[(4 *...  10.2 us
    all_to_all x1, starting transfers between devices, local(): parts = lax.all_to_all(part, 'band', 0, 0, tiled=True)  9.15 us
    ppermute x1, starting transfers between devices, local(): after = lax.ppermute(block, 'band', [(b + 1, b) for b in range(bands - 1)])  9.01 us
    ppermute x1, starting transfers between devices, local(): lax.ppermute(step_index, 'step', [((s + 1) % steps, s) for s in range(ste...  6.96 us
    all_to_all x1, waiting for transfers between devices, local(): parts = lax.all_to_all(part, 'band', 0, 0, tiled=True)  6.32 us
    pallas_call x1, Pallas kernels, local(): pl.pallas_call(denoise_kernel, out_shape=pltpu.VMEM((4, SUB, SPAN), BF16)...  3.75 us
    ppermute x1, starting transfers between devices, local(): before = lax.ppermute(block, 'band', [(b, b + 1) for b in range(bands - 1)])  1.92 us
  transfers between devices with their start and end apart: 8, of which 3 were waited for; matrix products, arithmetic and copies ran while one was open for 1% of the time, Pallas kernels for 3%

profile of v5, /device:TPU:1, one launch (start us, length us, event | category | flops | bytes accessed | tf_op | source)
XLA Modules:
  0.0 69.9 jit_solution(11781720079836742475)
XLA Ops:
  0.6 0.0 copy-start.7
  0.6 0.0 copy-start.6
  0.6 0.1 sight.1.sight_ref
  0.7 0.8 %copy-done.7 = f32[2,10752]{1,0:T(2,128)S(1)} copy-done((f32[2,10752]{1,0:T(2,128)S(1)}, f32[2,10752]{1,0:T(2,128)}, u32[]{:S(2)}) %copy-start.7) | copy-done | bytes 86040
  1.5 0.0 copy-done.6
  1.6 0.0 copy-start
  1.6 0.0 copy-start.4
  1.6 0.0 copy-start.8
  1.6 0.0 copy-start.9
  1.6 0.0 copy-start.2
  1.6 0.0 copy-start.1
  1.6 0.0 copy-start.3
  1.7 0.0 copy-start.5
  1.7 9.0 %collective-permute-start.1 = (bf16[8,2688]{1,0:T(8,128)(2,1)S(1)}, bf16[8,2688]{1,0:T(8,128)(2,1)S(1)}, u32[]{:S(2)}, u32[]{:S(2)}) collective-permute-start(bf16[8,2688]{1,0:T(8,128)(2,1)S(1)} %open.1.here_ref), channel_id=1, source_target_pairs={{1,0},{2,1},{3,2},{4,3},{5,4},{6,5},{7,6},{8,7},{9,8},{10,9},{11,1... | collective-permute-start | bytes 129032 | tf_op jit(solution)/shard_map/ppermute | solution.py:247
  10.7 1.9 %collective-permute-start = (bf16[8,2688]{1,0:T(8,128)(2,1)S(1)}, bf16[8,2688]{1,0:T(8,128)(2,1)S(1)}, u32[]{:S(2)}, u32[]{:S(2)}) collective-permute-start(bf16[8,2688]{1,0:T(8,128)(2,1)S(1)} %open.1.here_ref), channel_id=1, source_target_pairs={{0,1},{1,2},{2,3},{3,4},{4,5},{5,6},{6,7},{7,8},{8,9},{9,10},{10,1... | collective-permute-start | bytes 129032 | tf_op jit(solution)/shard_map/ppermute | solution.py:246
  12.6 7.0 %collective-permute-start.2 = (s32[1]{0:T(128)}, s32[1]{0:T(128)}, u32[]{:S(2)}, u32[]{:S(2)}) collective-permute-start(s32[1]{0:T(128)} %param.14), channel_id=1, source_target_pairs={{32,0},{64,32},{96,64},{128,96},{160,128},{192,160},{224,192},{256... | collective-permute-start | bytes 20 | tf_op jit(solution)/shard_map/ppermute | solution.py:245
  19.6 0.8 %collective-permute-done.2 = s32[1]{0:T(128)} collective-permute-done((s32[1]{0:T(128)}, s32[1]{0:T(128)}, u32[]{:S(2)}, u32[]{:S(2)}) %collective-permute-start.2) | collective-permute-done | bytes 36 | tf_op jit(solution)/shard_map/ppermute | solution.py:245
  20.4 0.0 copy-done
  20.4 0.0 copy-done.4
  20.4 0.0 copy-done.8
  20.4 0.0 copy-done.9
  20.4 1.9 %own.1 = (f32[256,512]{1,0:T(8,128)S(1)}, bf16[256,512]{1,0:T(8,128)(2,1)S(1)}, f32[4,256,1]{2,1,0:T(8,128)S(1)}, f32[4,256,128]{2,1,0:T(8,128)S(1)}, f32[1,512]{1,0:T(1,128)S(1)}, /*index=5*/f32[1,128]{1,0:T(1,128)S(1)}) custom-call(s32[1,1]{1,0:T(1,128)} %bitcast.index_ref, f32[1,20]{1,0:T(1,128)S(1)} %bitcast.10, f32[1,512]{1,0:T(1,128)S(1)} %bitcast.9, ...), custom_call_target="tpu_custom_call" | custom-call | tf_op jit(solution)/shard_map/own/pallas_call | solution.py:253
  22.3 0.0 collective-permute-done.1.after_ref
  22.3 0.0 collective-permute-done.before_ref
  22.4 0.0 copy-done.2
  22.4 0.0 copy-done.1
  22.4 0.0 copy-done.3
  22.4 0.0 copy-done.5
  22.4 0.0 copy-start.10
  22.4 3.8 %denoise.1 = bf16[4,8,2688]{2,1,0:T(8,128)(2,1)S(1)} custom-call(bf16[8,2688]{1,0:T(8,128)(2,1)S(1)} %collective-permute-done.before_ref, bf16[8,2688]{1,0:T(8,128)(2,1)S(1)} %collective-permute-done.1.after_ref, f32[256,512]{1,0:T(8,128)S(1)} %get-tuple-element.13.embedded_ref, bf16[256,512]{1,0:T(8,128)(2,1)S(1)} %get-tuple-element.14.queries_ref, ...), custom_call_target="tpu_custom_call" | custom-call | tf_op jit(solution)/shard_map/denoise/pallas_call | solution.py:263
  26.2 10.2 %all_to_all.14.group_ref = bf16[4,8,2688]{2,1,0:T(8,128)(2,1)S(1)} all-to-all(bf16[4,8,2688]{2,1,0:T(8,128)(2,1)S(1)} %denoise.1), channel_id=1, replica_groups={{480,0,32,64},{96,128,160,192},{224,256,288,320},{352,384,416,448},{481..., dimensions={0} | all-to-all | bytes 344064 | tf_op jit(solution)/shard_map/all_to_all | solution.py:270
  36.4 2.6 %collective-permute-start.3 = (bf16[8,2688]{1,0:T(8,128)(2,1)S(1)}, bf16[8,2688]{1,0:T(8,128)(2,1)S(1)}, u32[]{:S(2)}, u32[]{:S(2)}) collective-permute-start(bf16[8,2688]{1,0:T(8,128)(2,1)S(1)} %middle.1.sent_ref), channel_id=1, source_target_pairs={{480,96},{0,128},{32,160},{64,192},{96,224},{128,256},{160,288},{1... | collective-permute-start | bytes 129032 | tf_op jit(solution)/shard_map/ppermute | solution.py:281
  38.9 0.7 collective-permute-start.5
  39.6 9.4 %collective-permute-start.4 = (bf16[8,2688]{1,0:T(8,128)(2,1)S(1)}, bf16[8,2688]{1,0:T(8,128)(2,1)S(1)}, u32[]{:S(2)}, u32[]{:S(2)}) collective-permute-start(bf16[8,2688]{1,0:T(8,128)(2,1)S(1)} %middle.1.sent_ref), channel_id=1, source_target_pairs={{64,224},{32,256},{0,288},{480,320},{448,480},{65,225},{33,257},{1... | collective-permute-start | bytes 129032 | tf_op jit(solution)/shard_map/ppermute | solution.py:281
  49.0 0.0 collective-permute-done.3.near_ref
  49.0 0.7 collective-permute-start.6
  49.7 0.0 copy-done.10
  49.7 0.2 base.1
  49.9 0.0 collective-permute-done.5.next_ref
  49.9 0.8 %collective-permute-done.4.skip_ref = bf16[8,2688]{1,0:T(8,128)(2,1)S(1)} collective-permute-done((bf16[8,2688]{1,0:T(8,128)(2,1)S(1)}, bf16[8,2688]{1,0:T(8,128)(2,1)S(1)}, u32[]{:S(2)}, u32[]{:S(2)}) %collective-permute-start.4) | collective-permute-done | bytes 43040 | tf_op jit(solution)/shard_map/ppermute | solution.py:281
  50.7 0.0 collective-permute-done.6.pair_ref
  50.7 0.7 close.1
  51.3 9.1 %all-to-all-start.1 = ((f32[32,1,128]{2,1,0:T(1,128)}), f32[32,1,128]{2,1,0:T(1,128)S(1)}, u32[]{:S(2)}, u32[]{:S(2)}) async-start(f32[32,1,128]{2,1,0:T(1,128)} %bitcast.5), calls=%async_computation.1 | async-start | bytes 32768 | tf_op jit(solution)/shard_map/all_to_all | solution.py:303
  60.5 0.6 copy.15
  61.1 6.3 %all-to-all-done.1 = f32[32,1,128]{2,1,0:T(1,128)S(1)} async-done(((f32[32,1,128]{2,1,0:T(1,128)}), f32[32,1,128]{2,1,0:T(1,128)S(1)}, u32[]{:S(2)}, u32[]{:S(2)}) %all-to-all-start.1) | async-done | bytes 16416 | tf_op jit(solution)/shard_map/all_to_all | solution.py:303
  67.4 0.6 reduce_sum.9
  (3 shorter events, 0.1 us)
Async XLA Ops:
  0.6 0.9 %copy-start.7 = (f32[2,10752]{1,0:T(2,128)S(1)}, f32[2,10752]{1,0:T(2,128)}, u32[]{:S(2)}) copy-start(f32[2,10752]{1,0:T(2,128)} %anchor_ref.3) | copy-start | bytes 258052
  0.6 0.9 %copy-start.6 = (f32[1,2,10752]{2,1,0:T(2,128)S(1)}, f32[1,2,10752]{2,1,0:T(2,128)}, u32[]{:S(2)}) copy-start(f32[1,2,10752]{2,1,0:T(2,128)} %states_ref.3) | copy-start | bytes 258052
  1.6 18.9 %copy-start = (bf16[512,1536]{1,0:T(8,128)(2,1)S(1)}, bf16[512,1536]{1,0:T(8,128)(2,1)}, u32[]{:S(2)}) copy-start(bf16[512,1536]{1,0:T(8,128)(2,1)} %qkv_ref.3) | copy-start | bytes 4718596
  1.6 18.9 %copy-start.4 = (bf16[84,512]{1,0:T(8,128)(2,1)S(1)}, bf16[84,512]{1,0:T(8,128)(2,1)}, u32[]{:S(2)}) copy-start(bf16[84,512]{1,0:T(8,128)(2,1)} %enc_ref.3) | copy-start | bytes 258052
  1.6 18.9 %copy-start.8 = (f32[512]{0:T(512)S(1)}, f32[512]{0:T(512)}, u32[]{:S(2)}) copy-start(f32[512]{0:T(512)} %param.17) | copy-start | bytes 6148
  1.6 18.9 %copy-start.9 = (f32[20]{0:T(128)S(1)}, f32[20]{0:T(128)}, u32[]{:S(2)}) copy-start(f32[20]{0:T(128)} %param.15) | copy-start | bytes 244
  1.6 20.8 %copy-start.2 = (bf16[1024,512]{1,0:T(8,128)(2,1)S(1)}, bf16[1024,512]{1,0:T(8,128)(2,1)}, u32[]{:S(2)}) copy-start(bf16[1024,512]{1,0:T(8,128)(2,1)} %down_ref.1) | copy-start | bytes 3145732
  1.6 20.7 %copy-start.1 = (bf16[512,1024]{1,0:T(8,128)(2,1)S(1)}, bf16[512,1024]{1,0:T(8,128)(2,1)}, u32[]{:S(2)}) copy-start(bf16[512,1024]{1,0:T(8,128)(2,1)} %up_ref.1) | copy-start | bytes 3145732
  1.6 20.7 %copy-start.3 = (bf16[512,512]{1,0:T(8,128)(2,1)S(1)}, bf16[512,512]{1,0:T(8,128)(2,1)}, u32[]{:S(2)}) copy-start(bf16[512,512]{1,0:T(8,128)(2,1)} %out_w_ref.1) | copy-start | bytes 1572868
  1.7 20.7 %copy-start.5 = (bf16[512,84]{0,1:T(8,128)(2,1)S(1)}, bf16[512,84]{0,1:T(8,128)(2,1)}, u32[]{:S(2)}) copy-start(bf16[512,84]{0,1:T(8,128)(2,1)} %param.22) | copy-start | bytes 258052
  1.7 20.7 %collective-permute-start.1 = (bf16[8,2688]{1,0:T(8,128)(2,1)S(1)}, bf16[8,2688]{1,0:T(8,128)(2,1)S(1)}, u32[]{:S(2)}, u32[]{:S(2)}) collective-permute-start(bf16[8,2688]{1,0:T(8,128)(2,1)S(1)} %open.1.here_ref), channel_id=1, source_target_pairs={{1,0},{2,1},{3,2},{4,3},{5,4},{6,5},{7,6},{8,7},{9,8},{10,9},{11,1... | collective-permute-start | bytes 129032 | tf_op jit(solution)/shard_map/ppermute | solution.py:247
  10.7 11.7 %collective-permute-start = (bf16[8,2688]{1,0:T(8,128)(2,1)S(1)}, bf16[8,2688]{1,0:T(8,128)(2,1)S(1)}, u32[]{:S(2)}, u32[]{:S(2)}) collective-permute-start(bf16[8,2688]{1,0:T(8,128)(2,1)S(1)} %open.1.here_ref), channel_id=1, source_target_pairs={{0,1},{1,2},{2,3},{3,4},{4,5},{5,6},{6,7},{7,8},{8,9},{9,10},{10,1... | collective-permute-start | bytes 129032 | tf_op jit(solution)/shard_map/ppermute | solution.py:246
  12.6 7.8 %collective-permute-start.2 = (s32[1]{0:T(128)}, s32[1]{0:T(128)}, u32[]{:S(2)}, u32[]{:S(2)}) collective-permute-start(s32[1]{0:T(128)} %param.14), channel_id=1, source_target_pairs={{32,0},{64,32},{96,64},{128,96},{160,128},{192,160},{224,192},{256... | collective-permute-start | bytes 20 | tf_op jit(solution)/shard_map/ppermute | solution.py:245
  22.4 27.3 %copy-start.10 = (f32[1,64]{1,0:T(1,128)S(1)}, f32[1,64]{1,0:T(1,128)}, u32[]{:S(2)}) copy-start(f32[1,64]{1,0:T(1,128)} %constant.12.area_ref) | copy-start | bytes 772
  36.4 12.6 %collective-permute-start.3 = (bf16[8,2688]{1,0:T(8,128)(2,1)S(1)}, bf16[8,2688]{1,0:T(8,128)(2,1)S(1)}, u32[]{:S(2)}, u32[]{:S(2)}) collective-permute-start(bf16[8,2688]{1,0:T(8,128)(2,1)S(1)} %middle.1.sent_ref), channel_id=1, source_target_pairs={{480,96},{0,128},{32,160},{64,192},{96,224},{128,256},{160,288},{1... | collective-permute-start | bytes 129032 | tf_op jit(solution)/shard_map/ppermute | solution.py:281
  38.9 11.0 %collective-permute-start.5 = (bf16[8,2688]{1,0:T(8,128)(2,1)S(1)}, bf16[8,2688]{1,0:T(8,128)(2,1)S(1)}, u32[]{:S(2)}, u32[]{:S(2)}) collective-permute-start(bf16[8,2688]{1,0:T(8,128)(2,1)S(1)} %middle.1.sent_ref), channel_id=1, source_target_pairs={{224,352},{256,384},{288,416},{320,448},{225,353},{257,385},{289,4... | collective-permute-start | bytes 129032 | tf_op jit(solution)/shard_map/ppermute | solution.py:281
  39.6 11.1 %collective-permute-start.4 = (bf16[8,2688]{1,0:T(8,128)(2,1)S(1)}, bf16[8,2688]{1,0:T(8,128)(2,1)S(1)}, u32[]{:S(2)}, u32[]{:S(2)}) collective-permute-start(bf16[8,2688]{1,0:T(8,128)(2,1)S(1)} %middle.1.sent_ref), channel_id=1, source_target_pairs={{64,224},{32,256},{0,288},{480,320},{448,480},{65,225},{33,257},{1... | collective-permute-start | bytes 129032 | tf_op jit(solution)/shard_map/ppermute | solution.py:281
  49.0 1.6 %collective-permute-start.6 = (bf16[8,2688]{1,0:T(8,128)(2,1)S(1)}, bf16[8,2688]{1,0:T(8,128)(2,1)S(1)}, u32[]{:S(2)}, u32[]{:S(2)}) collective-permute-start(bf16[8,2688]{1,0:T(8,128)(2,1)S(1)} %both.1), channel_id=1, source_target_pairs={{192,352},{160,384},{128,416},{96,448},{320,480},{193,353},{161,38... | collective-permute-start | bytes 129032 | tf_op jit(solution)/shard_map/ppermute | solution.py:281
  51.3 16.1 %all-to-all-start.1 = ((f32[32,1,128]{2,1,0:T(1,128)}), f32[32,1,128]{2,1,0:T(1,128)S(1)}, u32[]{:S(2)}, u32[]{:S(2)}) async-start(f32[32,1,128]{2,1,0:T(1,128)} %bitcast.5), calls=%async_computation.1 | async-start | bytes 32768 | tf_op jit(solution)/shard_map/all_to_all | solution.py:303

commit v6 on v5

--- a/solution.py
+++ b/solution.py
@@ -176,13 +176,15 @@
         copies_ref[i] = packed
 
 
-def middle_kernel(group_ref, sent_ref):
+def middle_kernel(group_ref, sent_ref, total_ref):
     parts = [group_ref[i].astype(F32) for i in range(4)]
-    sent_ref[...] = ((parts[0] + parts[1]) + (parts[2] + parts[3])).astype(BF16)
-
-
-def both_kernel(sent_ref, near_ref, both_ref):
-    both_ref[...] = (sent_ref[...].astype(F32) + near_ref[...].astype(F32)).astype(BF16)
+    total = (parts[0] + parts[1]) + (parts[2] + parts[3])
+    total_ref[...] = total
+    sent_ref[...] = total.astype(BF16)
+
+
+def both_kernel(total_ref, near_ref, both_ref):
+    both_ref[...] = total_ref[...] + near_ref[...].astype(F32)
 
 
 def base_kernel(group_ref, anchor_ref, states_ref, area_ref, base_ref, old_ref, scale_ref):
@@ -206,7 +208,7 @@
 ):
     new = base_ref[...] + (
         (near_ref[...].astype(F32) + next_ref[...].astype(F32))
-        + (skip_ref[...].astype(F32) + pair_ref[...].astype(F32))
+        + (skip_ref[...].astype(F32) + pair_ref[...])
     )
     for g in range(PACKS):
         new_ref[0, :, g * SPAN : (g + 1) * SPAN] = new[2 * g : 2 * g + 2, :]
@@ -272,8 +274,9 @@
         axis_index_groups=[[(4 * g + i - 1) % steps for i in range(4)] for g in range(steps // 4)],
     )
     packed = pltpu.VMEM((SUB, SPAN), F32)
-    sent = pl.pallas_call(
-        middle_kernel, out_shape=pltpu.VMEM((SUB, SPAN), BF16), in_specs=[vmem], out_specs=vmem,
+    sent, total = pl.pallas_call(
+        middle_kernel, out_shape=(pltpu.VMEM((SUB, SPAN), BF16), packed), in_specs=[vmem],
+        out_specs=(vmem, vmem),
         name="middle", compiler_params=limit(8),
     )(*local_vmem(group))
 
@@ -284,9 +287,9 @@
     skip = moved(sent, SKIP)
     following = moved(sent, NEXT)
     both = pl.pallas_call(
-        both_kernel, out_shape=pltpu.VMEM((SUB, SPAN), BF16), in_specs=[vmem] * 2, out_specs=vmem,
+        both_kernel, out_shape=packed, in_specs=[vmem] * 2, out_specs=vmem,
         name="both", compiler_params=limit(8),
-    )(*local_vmem(sent, near))
+    )(*local_vmem(total, near))
     pair = moved(both, PAIR)
     far = (near, skip, following, pair)
     latitude = np.pi * ((np.arange(NLAT, dtype=np.float32) + 0.5) / NLAT - 0.5)

time: 70.2 us -> 78.2 us (1.11)
  starting transfers between devices: 40.3 us -> 47 us
  waiting for transfers between devices: 7.95 us -> 9.18 us
    ppermute x4, starting transfers between devices: 13.3 us -> 17.1 us  [moved(): return lax.ppermute(array, 'step', pairs)]
    all_to_all x1, starting transfers between devices: 9.15 us -> 12 us  [local(): parts = lax.all_to_all(part, 'band', 0, 0, tiled=True)]
    ppermute x4, waiting for transfers between devices: 0.79 us -> 2.02 us  [moved(): return lax.ppermute(array, 'step', pairs)]
  transfers between devices with their start and end apart: 8 -> 8, of which waited for: 3 -> 4; matrix products, arithmetic and copies ran while one was open for 1% -> 1% of each run, Pallas kernels for 3% -> 3%
where the time goes in v6:
time: 78.2 us; the launch traced here: 77.8 us
  starting transfers between devices  47 us (60%)
  blocking collectives  10.2 us (13%)
  waiting for transfers between devices  9.18 us (12%)
  Pallas kernels  6.7 us (9%)
  between operations  2.63 us (3%)
  local copies, waits for them, and re-layouts  1.52 us (2%)
    ppermute x4, starting transfers between devices, moved(): return lax.ppermute(array, 'step', pairs)  17.1 us
    all_to_all x1, starting transfers between devices, local(): parts = lax.all_to_all(part, 'band', 0, 0, tiled=True)  12 us
    all_to_all x1, blocking collectives, local(): lax.all_to_all(copies, 'step', 0, 0, tiled=True, axis_index_groups=[[(4 *...  10.2 us
    ppermute x1, starting transfers between devices, local(): after = lax.ppermute(block, 'band', [(b + 1, b) for b in range(bands - 1)])  9.01 us
    ppermute x1, starting transfers between devices, local(): lax.ppermute(step_index, 'step', [((s + 1) % steps, s) for s in range(ste...  6.96 us
    all_to_all x1, waiting for transfers between devices, local(): parts = lax.all_to_all(part, 'band', 0, 0, tiled=True)  6.32 us
    pallas_call x1, Pallas kernels, local(): pl.pallas_call(denoise_kernel, out_shape=pltpu.VMEM((4, SUB, SPAN), BF16)...  3.75 us
    ppermute x4, waiting for transfers between devices, moved(): return lax.ppermute(array, 'step', pairs)  2.02 us
  transfers between devices with their start and end apart: 8, of which 4 were waited for; matrix products, arithmetic and copies ran while one was open for 1% of the time, Pallas kernels for 3%

profile of v6, /device:TPU:1, one launch (start us, length us, event | category | flops | bytes accessed | tf_op | source)
XLA Modules:
  0.0 77.8 jit_solution(16601945851012732152)
XLA Ops:
  0.6 0.0 copy-start.7
  0.6 0.0 copy-start.6
  0.6 0.1 sight.1.sight_ref
  0.7 0.8 %copy-done.7 = f32[2,10752]{1,0:T(2,128)S(1)} copy-done((f32[2,10752]{1,0:T(2,128)S(1)}, f32[2,10752]{1,0:T(2,128)}, u32[]{:S(2)}) %copy-start.7) | copy-done | bytes 86040
  1.5 0.0 copy-done.6
  1.6 0.0 copy-start
  1.6 0.0 copy-start.4
  1.6 0.0 copy-start.8
  1.6 0.0 copy-start.9
  1.6 0.0 copy-start.2
  1.6 0.0 copy-start.1
  1.6 0.0 copy-start.3
  1.7 0.0 copy-start.5
  1.7 9.0 %collective-permute-start.1 = (bf16[8,2688]{1,0:T(8,128)(2,1)S(1)}, bf16[8,2688]{1,0:T(8,128)(2,1)S(1)}, u32[]{:S(2)}, u32[]{:S(2)}) collective-permute-start(bf16[8,2688]{1,0:T(8,128)(2,1)S(1)} %open.1.here_ref), channel_id=1, source_target_pairs={{1,0},{2,1},{3,2},{4,3},{5,4},{6,5},{7,6},{8,7},{9,8},{10,9},{11,1... | collective-permute-start | bytes 129032 | tf_op jit(solution)/shard_map/ppermute | solution.py:249
  10.7 1.9 %collective-permute-start = (bf16[8,2688]{1,0:T(8,128)(2,1)S(1)}, bf16[8,2688]{1,0:T(8,128)(2,1)S(1)}, u32[]{:S(2)}, u32[]{:S(2)}) collective-permute-start(bf16[8,2688]{1,0:T(8,128)(2,1)S(1)} %open.1.here_ref), channel_id=1, source_target_pairs={{0,1},{1,2},{2,3},{3,4},{4,5},{5,6},{6,7},{7,8},{8,9},{9,10},{10,1... | collective-permute-start | bytes 129032 | tf_op jit(solution)/shard_map/ppermute | solution.py:248
  12.6 7.0 %collective-permute-start.2 = (s32[1]{0:T(128)}, s32[1]{0:T(128)}, u32[]{:S(2)}, u32[]{:S(2)}) collective-permute-start(s32[1]{0:T(128)} %param.14), channel_id=1, source_target_pairs={{32,0},{64,32},{96,64},{128,96},{160,128},{192,160},{224,192},{256... | collective-permute-start | bytes 20 | tf_op jit(solution)/shard_map/ppermute | solution.py:247
  19.6 0.8 %collective-permute-done.2 = s32[1]{0:T(128)} collective-permute-done((s32[1]{0:T(128)}, s32[1]{0:T(128)}, u32[]{:S(2)}, u32[]{:S(2)}) %collective-permute-start.2) | collective-permute-done | bytes 36 | tf_op jit(solution)/shard_map/ppermute | solution.py:247
  20.4 0.0 copy-done
  20.4 0.0 copy-done.4
  20.4 0.0 copy-done.8
  20.4 0.0 copy-done.9
  20.4 2.0 %own.1 = (f32[256,512]{1,0:T(8,128)S(1)}, bf16[256,512]{1,0:T(8,128)(2,1)S(1)}, f32[4,256,1]{2,1,0:T(8,128)S(1)}, f32[4,256,128]{2,1,0:T(8,128)S(1)}, f32[1,512]{1,0:T(1,128)S(1)}, /*index=5*/f32[1,128]{1,0:T(1,128)S(1)}) custom-call(s32[1,1]{1,0:T(1,128)} %bitcast.index_ref, f32[1,20]{1,0:T(1,128)S(1)} %bitcast.10, f32[1,512]{1,0:T(1,128)S(1)} %bitcast.9, ...), custom_call_target="tpu_custom_call" | custom-call | tf_op jit(solution)/shard_map/own/pallas_call | solution.py:255
  22.4 0.0 collective-permute-done.1.after_ref
  22.4 0.0 collective-permute-done.before_ref
  22.4 0.0 copy-done.2
  22.4 0.0 copy-done.1
  22.4 0.0 copy-done.3
  22.4 0.0 copy-done.5
  22.5 0.0 copy-start.10
  22.5 3.7 %denoise.1 = bf16[4,8,2688]{2,1,0:T(8,128)(2,1)S(1)} custom-call(bf16[8,2688]{1,0:T(8,128)(2,1)S(1)} %collective-permute-done.before_ref, bf16[8,2688]{1,0:T(8,128)(2,1)S(1)} %collective-permute-done.1.after_ref, f32[256,512]{1,0:T(8,128)S(1)} %get-tuple-element.15.embedded_ref, bf16[256,512]{1,0:T(8,128)(2,1)S(1)} %get-tuple-element.16.queries_ref, ...), custom_call_target="tpu_custom_call" | custom-call | tf_op jit(solution)/shard_map/denoise/pallas_call | solution.py:265
  26.2 10.2 %all_to_all.14.group_ref = bf16[4,8,2688]{2,1,0:T(8,128)(2,1)S(1)} all-to-all(bf16[4,8,2688]{2,1,0:T(8,128)(2,1)S(1)} %denoise.1), channel_id=1, replica_groups={{480,0,32,64},{96,128,160,192},{224,256,288,320},{352,384,416,448},{481..., dimensions={0} | all-to-all | bytes 344064 | tf_op jit(solution)/shard_map/all_to_all | solution.py:272
  36.4 2.6 %collective-permute-start.3 = (bf16[8,2688]{1,0:T(8,128)(2,1)S(1)}, bf16[8,2688]{1,0:T(8,128)(2,1)S(1)}, u32[]{:S(2)}, u32[]{:S(2)}) collective-permute-start(bf16[8,2688]{1,0:T(8,128)(2,1)S(1)} %get-tuple-element.21), channel_id=1, source_target_pairs={{480,96},{0,128},{32,160},{64,192},{96,224},{128,256},{160,288},{1... | collective-permute-start | bytes 129032 | tf_op jit(solution)/shard_map/ppermute | solution.py:284
  39.0 1.1 %collective-permute-done.3.near_ref = bf16[8,2688]{1,0:T(8,128)(2,1)S(1)} collective-permute-done((bf16[8,2688]{1,0:T(8,128)(2,1)S(1)}, bf16[8,2688]{1,0:T(8,128)(2,1)S(1)}, u32[]{:S(2)}, u32[]{:S(2)}) %collective-permute-start.3) | collective-permute-done | bytes 43040 | tf_op jit(solution)/shard_map/ppermute | solution.py:284
  40.1 0.7 collective-permute-start.6
  40.8 0.7 collective-permute-start.5
  41.5 13.2 %collective-permute-start.4 = (bf16[8,2688]{1,0:T(8,128)(2,1)S(1)}, bf16[8,2688]{1,0:T(8,128)(2,1)S(1)}, u32[]{:S(2)}, u32[]{:S(2)}) collective-permute-start(bf16[8,2688]{1,0:T(8,128)(2,1)S(1)} %get-tuple-element.21), channel_id=1, source_target_pairs={{64,224},{32,256},{0,288},{480,320},{448,480},{65,225},{33,257},{1... | collective-permute-start | bytes 129032 | tf_op jit(solution)/shard_map/ppermute | solution.py:284
  54.7 0.0 copy-done.10
  54.7 0.2 base.1
  54.8 0.0 collective-permute-done.5.next_ref
  54.8 0.9 %collective-permute-done.4.skip_ref = bf16[8,2688]{1,0:T(8,128)(2,1)S(1)} collective-permute-done((bf16[8,2688]{1,0:T(8,128)(2,1)S(1)}, bf16[8,2688]{1,0:T(8,128)(2,1)S(1)}, u32[]{:S(2)}, u32[]{:S(2)}) %collective-permute-start.4) | collective-permute-done | bytes 43040 | tf_op jit(solution)/shard_map/ppermute | solution.py:284
  55.8 0.0 collective-permute-done.6.pair_ref
  55.8 0.7 close.1
  56.4 12.0 %all-to-all-start.1 = ((f32[32,1,128]{2,1,0:T(1,128)}), f32[32,1,128]{2,1,0:T(1,128)S(1)}, u32[]{:S(2)}, u32[]{:S(2)}) async-start(f32[32,1,128]{2,1,0:T(1,128)} %bitcast.5), calls=%async_computation.1 | async-start | bytes 32768 | tf_op jit(solution)/shard_map/all_to_all | solution.py:306
  68.4 0.6 copy.15
  69.1 6.3 %all-to-all-done.1 = f32[32,1,128]{2,1,0:T(1,128)S(1)} async-done(((f32[32,1,128]{2,1,0:T(1,128)}), f32[32,1,128]{2,1,0:T(1,128)S(1)}, u32[]{:S(2)}, u32[]{:S(2)}) %all-to-all-start.1) | async-done | bytes 16416 | tf_op jit(solution)/shard_map/all_to_all | solution.py:306
  75.4 0.6 reduce_sum.9
  (3 shorter events, 0.1 us)
Async XLA Ops:
  0.6 0.9 %copy-start.7 = (f32[2,10752]{1,0:T(2,128)S(1)}, f32[2,10752]{1,0:T(2,128)}, u32[]{:S(2)}) copy-start(f32[2,10752]{1,0:T(2,128)} %anchor_ref.3) | copy-start | bytes 258052
  0.6 0.9 %copy-start.6 = (f32[1,2,10752]{2,1,0:T(2,128)S(1)}, f32[1,2,10752]{2,1,0:T(2,128)}, u32[]{:S(2)}) copy-start(f32[1,2,10752]{2,1,0:T(2,128)} %states_ref.3) | copy-start | bytes 258052
  1.6 18.9 %copy-start = (bf16[512,1536]{1,0:T(8,128)(2,1)S(1)}, bf16[512,1536]{1,0:T(8,128)(2,1)}, u32[]{:S(2)}) copy-start(bf16[512,1536]{1,0:T(8,128)(2,1)} %qkv_ref.3) | copy-start | bytes 4718596
  1.6 18.9 %copy-start.4 = (bf16[84,512]{1,0:T(8,128)(2,1)S(1)}, bf16[84,512]{1,0:T(8,128)(2,1)}, u32[]{:S(2)}) copy-start(bf16[84,512]{1,0:T(8,128)(2,1)} %enc_ref.3) | copy-start | bytes 258052
  1.6 18.9 %copy-start.8 = (f32[512]{0:T(512)S(1)}, f32[512]{0:T(512)}, u32[]{:S(2)}) copy-start(f32[512]{0:T(512)} %param.17) | copy-start | bytes 6148
  1.6 18.9 %copy-start.9 = (f32[20]{0:T(128)S(1)}, f32[20]{0:T(128)}, u32[]{:S(2)}) copy-start(f32[20]{0:T(128)} %param.15) | copy-start | bytes 244
  1.6 20.8 %copy-start.2 = (bf16[1024,512]{1,0:T(8,128)(2,1)S(1)}, bf16[1024,512]{1,0:T(8,128)(2,1)}, u32[]{:S(2)}) copy-start(bf16[1024,512]{1,0:T(8,128)(2,1)} %down_ref.1) | copy-start | bytes 3145732
  1.6 20.8 %copy-start.1 = (bf16[512,1024]{1,0:T(8,128)(2,1)S(1)}, bf16[512,1024]{1,0:T(8,128)(2,1)}, u32[]{:S(2)}) copy-start(bf16[512,1024]{1,0:T(8,128)(2,1)} %up_ref.1) | copy-start | bytes 3145732
  1.6 20.8 %copy-start.3 = (bf16[512,512]{1,0:T(8,128)(2,1)S(1)}, bf16[512,512]{1,0:T(8,128)(2,1)}, u32[]{:S(2)}) copy-start(bf16[512,512]{1,0:T(8,128)(2,1)} %out_w_ref.1) | copy-start | bytes 1572868
  1.7 20.8 %copy-start.5 = (bf16[512,84]{0,1:T(8,128)(2,1)S(1)}, bf16[512,84]{0,1:T(8,128)(2,1)}, u32[]{:S(2)}) copy-start(bf16[512,84]{0,1:T(8,128)(2,1)} %param.22) | copy-start | bytes 258052
  1.7 20.7 %collective-permute-start.1 = (bf16[8,2688]{1,0:T(8,128)(2,1)S(1)}, bf16[8,2688]{1,0:T(8,128)(2,1)S(1)}, u32[]{:S(2)}, u32[]{:S(2)}) collective-permute-start(bf16[8,2688]{1,0:T(8,128)(2,1)S(1)} %open.1.here_ref), channel_id=1, source_target_pairs={{1,0},{2,1},{3,2},{4,3},{5,4},{6,5},{7,6},{8,7},{9,8},{10,9},{11,1... | collective-permute-start | bytes 129032 | tf_op jit(solution)/shard_map/ppermute | solution.py:249
  10.7 11.7 %collective-permute-start = (bf16[8,2688]{1,0:T(8,128)(2,1)S(1)}, bf16[8,2688]{1,0:T(8,128)(2,1)S(1)}, u32[]{:S(2)}, u32[]{:S(2)}) collective-permute-start(bf16[8,2688]{1,0:T(8,128)(2,1)S(1)} %open.1.here_ref), channel_id=1, source_target_pairs={{0,1},{1,2},{2,3},{3,4},{4,5},{5,6},{6,7},{7,8},{8,9},{9,10},{10,1... | collective-permute-start | bytes 129032 | tf_op jit(solution)/shard_map/ppermute | solution.py:248
  12.6 7.8 %collective-permute-start.2 = (s32[1]{0:T(128)}, s32[1]{0:T(128)}, u32[]{:S(2)}, u32[]{:S(2)}) collective-permute-start(s32[1]{0:T(128)} %param.14), channel_id=1, source_target_pairs={{32,0},{64,32},{96,64},{128,96},{160,128},{192,160},{224,192},{256... | collective-permute-start | bytes 20 | tf_op jit(solution)/shard_map/ppermute | solution.py:247
  22.5 32.2 %copy-start.10 = (f32[1,64]{1,0:T(1,128)S(1)}, f32[1,64]{1,0:T(1,128)}, u32[]{:S(2)}) copy-start(f32[1,64]{1,0:T(1,128)} %constant.12.area_ref) | copy-start | bytes 772
  36.4 3.7 %collective-permute-start.3 = (bf16[8,2688]{1,0:T(8,128)(2,1)S(1)}, bf16[8,2688]{1,0:T(8,128)(2,1)S(1)}, u32[]{:S(2)}, u32[]{:S(2)}) collective-permute-start(bf16[8,2688]{1,0:T(8,128)(2,1)S(1)} %get-tuple-element.21), channel_id=1, source_target_pairs={{480,96},{0,128},{32,160},{64,192},{96,224},{128,256},{160,288},{1... | collective-permute-start | bytes 129032 | tf_op jit(solution)/shard_map/ppermute | solution.py:284
  40.1 15.6 %collective-permute-start.6 = (f32[8,2688]{1,0:T(8,128)S(1)}, f32[8,2688]{1,0:T(8,128)S(1)}, u32[]{:S(2)}, u32[]{:S(2)}) collective-permute-start(f32[8,2688]{1,0:T(8,128)S(1)} %both.1), channel_id=1, source_target_pairs={{192,352},{160,384},{128,416},{96,448},{320,480},{193,353},{161,38... | collective-permute-start | bytes 258056 | tf_op jit(solution)/shard_map/ppermute | solution.py:284
  40.8 14.1 %collective-permute-start.5 = (bf16[8,2688]{1,0:T(8,128)(2,1)S(1)}, bf16[8,2688]{1,0:T(8,128)(2,1)S(1)}, u32[]{:S(2)}, u32[]{:S(2)}) collective-permute-start(bf16[8,2688]{1,0:T(8,128)(2,1)S(1)} %get-tuple-element.21), channel_id=1, source_target_pairs={{224,352},{256,384},{288,416},{320,448},{225,353},{257,385},{289,4... | collective-permute-start | bytes 129032 | tf_op jit(solution)/shard_map/ppermute | solution.py:284
  41.5 14.3 %collective-permute-start.4 = (bf16[8,2688]{1,0:T(8,128)(2,1)S(1)}, bf16[8,2688]{1,0:T(8,128)(2,1)S(1)}, u32[]{:S(2)}, u32[]{:S(2)}) collective-permute-start(bf16[8,2688]{1,0:T(8,128)(2,1)S(1)} %get-tuple-element.21), channel_id=1, source_target_pairs={{64,224},{32,256},{0,288},{480,320},{448,480},{65,225},{33,257},{1... | collective-permute-start | bytes 129032 | tf_op jit(solution)/shard_map/ppermute | solution.py:284
  56.4 19.0 %all-to-all-start.1 = ((f32[32,1,128]{2,1,0:T(1,128)}), f32[32,1,128]{2,1,0:T(1,128)S(1)}, u32[]{:S(2)}, u32[]{:S(2)}) async-start(f32[32,1,128]{2,1,0:T(1,128)} %bitcast.5), calls=%async_computation.1 | async-start | bytes 32768 | tf_op jit(solution)/shard_map/all_to_all | solution.py:306

commit v7 on v6

--- a/solution.py
+++ b/solution.py
@@ -184,7 +184,7 @@
 
 
 def both_kernel(total_ref, near_ref, both_ref):
-    both_ref[...] = total_ref[...] + near_ref[...].astype(F32)
+    both_ref[...] = (total_ref[...] + near_ref[...].astype(F32)).astype(BF16)
 
 
 def base_kernel(group_ref, anchor_ref, states_ref, area_ref, base_ref, old_ref, scale_ref):
@@ -208,7 +208,7 @@
 ):
     new = base_ref[...] + (
         (near_ref[...].astype(F32) + next_ref[...].astype(F32))
-        + (skip_ref[...].astype(F32) + pair_ref[...])
+        + (skip_ref[...].astype(F32) + pair_ref[...].astype(F32))
     )
     for g in range(PACKS):
         new_ref[0, :, g * SPAN : (g + 1) * SPAN] = new[2 * g : 2 * g + 2, :]
@@ -287,7 +287,7 @@
     skip = moved(sent, SKIP)
     following = moved(sent, NEXT)
     both = pl.pallas_call(
-        both_kernel, out_shape=packed, in_specs=[vmem] * 2, out_specs=vmem,
+        both_kernel, out_shape=pltpu.VMEM((SUB, SPAN), BF16), in_specs=[vmem] * 2, out_specs=vmem,
         name="both", compiler_params=limit(8),
     )(*local_vmem(total, near))
     pair = moved(both, PAIR)

time: 78.2 us -> 70.3 us (0.90)
  starting transfers between devices: 47 us -> 40.3 us
  waiting for transfers between devices: 9.18 us -> 7.95 us
    ppermute x4, starting transfers between devices: 17.1 us -> 13.3 us  [moved(): return lax.ppermute(array, 'step', pairs)]
    all_to_all x1, starting transfers between devices: 12 us -> 9.15 us  [local(): parts = lax.all_to_all(part, 'band', 0, 0, tiled=True)]
    ppermute x4, waiting for transfers between devices: 2.02 us -> 0.79 us  [moved(): return lax.ppermute(array, 'step', pairs)]
  transfers between devices with their start and end apart: 8 -> 8, of which waited for: 4 -> 3; matrix products, arithmetic and copies ran while one was open for 1% -> 1% of each run, Pallas kernels for 3% -> 3%
where the time goes in v7:
time: 70.3 us; the launch traced here: 69.9 us
  starting transfers between devices  40.3 us (57%)
  blocking collectives  10.2 us (15%)
  waiting for transfers between devices  7.95 us (11%)
  Pallas kernels  6.7 us (10%)
  between operations  2.64 us (4%)
  local copies, waits for them, and re-layouts  1.52 us (2%)
    ppermute x4, starting transfers between devices, moved(): return lax.ppermute(array, 'step', pairs)  13.3 us
    all_to_all x1, blocking collectives, local(): lax.all_to_all(copies, 'step', 0, 0, tiled=True, axis_index_groups=[[(4 *...  10.2 us
    all_to_all x1, starting transfers between devices, local(): parts = lax.all_to_all(part, 'band', 0, 0, tiled=True)  9.15 us
    ppermute x1, starting transfers between devices, local(): after = lax.ppermute(block, 'band', [(b + 1, b) for b in range(bands - 1)])  9.01 us
    ppermute x1, starting transfers between devices, local(): lax.ppermute(step_index, 'step', [((s + 1) % steps, s) for s in range(ste...  6.96 us
    all_to_all x1, waiting for transfers between devices, local(): parts = lax.all_to_all(part, 'band', 0, 0, tiled=True)  6.32 us
    pallas_call x1, Pallas kernels, local(): pl.pallas_call(denoise_kernel, out_shape=pltpu.VMEM((4, SUB, SPAN), BF16)...  3.75 us
    pallas_call x1, Pallas kernels, local(): pl.pallas_call(own_kernel, out_shape=(pltpu.VMEM((TOK, W), F32), pltpu.VM...  1.96 us
  transfers between devices with their start and end apart: 8, of which 3 were waited for; matrix products, arithmetic and copies ran while one was open for 1% of the time, Pallas kernels for 3%

profile of v7, /device:TPU:1, one launch (start us, length us, event | category | flops | bytes accessed | tf_op | source)
XLA Modules:
  0.0 69.9 jit_solution(7239237006881114176)
XLA Ops:
  0.6 0.0 copy-start.7
  0.6 0.0 copy-start.6
  0.6 0.1 sight.1.sight_ref
  0.7 0.8 %copy-done.7 = f32[2,10752]{1,0:T(2,128)S(1)} copy-done((f32[2,10752]{1,0:T(2,128)S(1)}, f32[2,10752]{1,0:T(2,128)}, u32[]{:S(2)}) %copy-start.7) | copy-done | bytes 86040
  1.5 0.0 copy-done.6
  1.6 0.0 copy-start
  1.6 0.0 copy-start.4
  1.6 0.0 copy-start.8
  1.6 0.0 copy-start.9
  1.6 0.0 copy-start.2
  1.6 0.0 copy-start.1
  1.6 0.0 copy-start.3
  1.7 0.0 copy-start.5
  1.7 9.0 %collective-permute-start.1 = (bf16[8,2688]{1,0:T(8,128)(2,1)S(1)}, bf16[8,2688]{1,0:T(8,128)(2,1)S(1)}, u32[]{:S(2)}, u32[]{:S(2)}) collective-permute-start(bf16[8,2688]{1,0:T(8,128)(2,1)S(1)} %open.1.here_ref), channel_id=1, source_target_pairs={{1,0},{2,1},{3,2},{4,3},{5,4},{6,5},{7,6},{8,7},{9,8},{10,9},{11,1... | collective-permute-start | bytes 129032 | tf_op jit(solution)/shard_map/ppermute | solution.py:249
  10.7 1.9 %collective-permute-start = (bf16[8,2688]{1,0:T(8,128)(2,1)S(1)}, bf16[8,2688]{1,0:T(8,128)(2,1)S(1)}, u32[]{:S(2)}, u32[]{:S(2)}) collective-permute-start(bf16[8,2688]{1,0:T(8,128)(2,1)S(1)} %open.1.here_ref), channel_id=1, source_target_pairs={{0,1},{1,2},{2,3},{3,4},{4,5},{5,6},{6,7},{7,8},{8,9},{9,10},{10,1... | collective-permute-start | bytes 129032 | tf_op jit(solution)/shard_map/ppermute | solution.py:248
  12.6 7.0 %collective-permute-start.2 = (s32[1]{0:T(128)}, s32[1]{0:T(128)}, u32[]{:S(2)}, u32[]{:S(2)}) collective-permute-start(s32[1]{0:T(128)} %param.14), channel_id=1, source_target_pairs={{32,0},{64,32},{96,64},{128,96},{160,128},{192,160},{224,192},{256... | collective-permute-start | bytes 20 | tf_op jit(solution)/shard_map/ppermute | solution.py:247
  19.6 0.8 %collective-permute-done.2 = s32[1]{0:T(128)} collective-permute-done((s32[1]{0:T(128)}, s32[1]{0:T(128)}, u32[]{:S(2)}, u32[]{:S(2)}) %collective-permute-start.2) | collective-permute-done | bytes 36 | tf_op jit(solution)/shard_map/ppermute | solution.py:247
  20.4 0.0 copy-done
  20.4 0.0 copy-done.4
  20.4 0.0 copy-done.8
  20.4 0.0 copy-done.9
  20.4 2.0 %own.1 = (f32[256,512]{1,0:T(8,128)S(1)}, bf16[256,512]{1,0:T(8,128)(2,1)S(1)}, f32[4,256,1]{2,1,0:T(8,128)S(1)}, f32[4,256,128]{2,1,0:T(8,128)S(1)}, f32[1,512]{1,0:T(1,128)S(1)}, /*index=5*/f32[1,128]{1,0:T(1,128)S(1)}) custom-call(s32[1,1]{1,0:T(1,128)} %bitcast.index_ref, f32[1,20]{1,0:T(1,128)S(1)} %bitcast.10, f32[1,512]{1,0:T(1,128)S(1)} %bitcast.9, ...), custom_call_target="tpu_custom_call" | custom-call | tf_op jit(solution)/shard_map/own/pallas_call | solution.py:255
  22.4 0.0 collective-permute-done.1.after_ref
  22.4 0.0 collective-permute-done.before_ref
  22.4 0.0 copy-done.2
  22.4 0.0 copy-done.1
  22.4 0.0 copy-done.3
  22.4 0.0 copy-done.5
  22.5 0.0 copy-start.10
  22.5 3.7 %denoise.1 = bf16[4,8,2688]{2,1,0:T(8,128)(2,1)S(1)} custom-call(bf16[8,2688]{1,0:T(8,128)(2,1)S(1)} %collective-permute-done.before_ref, bf16[8,2688]{1,0:T(8,128)(2,1)S(1)} %collective-permute-done.1.after_ref, f32[256,512]{1,0:T(8,128)S(1)} %get-tuple-element.15.embedded_ref, bf16[256,512]{1,0:T(8,128)(2,1)S(1)} %get-tuple-element.16.queries_ref, ...), custom_call_target="tpu_custom_call" | custom-call | tf_op jit(solution)/shard_map/denoise/pallas_call | solution.py:265
  26.2 10.2 %all_to_all.14.group_ref = bf16[4,8,2688]{2,1,0:T(8,128)(2,1)S(1)} all-to-all(bf16[4,8,2688]{2,1,0:T(8,128)(2,1)S(1)} %denoise.1), channel_id=1, replica_groups={{480,0,32,64},{96,128,160,192},{224,256,288,320},{352,384,416,448},{481..., dimensions={0} | all-to-all | bytes 344064 | tf_op jit(solution)/shard_map/all_to_all | solution.py:272
  36.4 2.6 %collective-permute-start.3 = (bf16[8,2688]{1,0:T(8,128)(2,1)S(1)}, bf16[8,2688]{1,0:T(8,128)(2,1)S(1)}, u32[]{:S(2)}, u32[]{:S(2)}) collective-permute-start(bf16[8,2688]{1,0:T(8,128)(2,1)S(1)} %get-tuple-element.21), channel_id=1, source_target_pairs={{480,96},{0,128},{32,160},{64,192},{96,224},{128,256},{160,288},{1... | collective-permute-start | bytes 129032 | tf_op jit(solution)/shard_map/ppermute | solution.py:284
  39.0 0.7 collective-permute-start.5
  39.7 9.4 %collective-permute-start.4 = (bf16[8,2688]{1,0:T(8,128)(2,1)S(1)}, bf16[8,2688]{1,0:T(8,128)(2,1)S(1)}, u32[]{:S(2)}, u32[]{:S(2)}) collective-permute-start(bf16[8,2688]{1,0:T(8,128)(2,1)S(1)} %get-tuple-element.21), channel_id=1, source_target_pairs={{64,224},{32,256},{0,288},{480,320},{448,480},{65,225},{33,257},{1... | collective-permute-start | bytes 129032 | tf_op jit(solution)/shard_map/ppermute | solution.py:284
  49.1 0.0 collective-permute-done.3.near_ref
  49.1 0.7 collective-permute-start.6
  49.8 0.0 copy-done.10
  49.8 0.2 base.1
  49.9 0.0 collective-permute-done.5.next_ref
  49.9 0.8 %collective-permute-done.4.skip_ref = bf16[8,2688]{1,0:T(8,128)(2,1)S(1)} collective-permute-done((bf16[8,2688]{1,0:T(8,128)(2,1)S(1)}, bf16[8,2688]{1,0:T(8,128)(2,1)S(1)}, u32[]{:S(2)}, u32[]{:S(2)}) %collective-permute-start.4) | collective-permute-done | bytes 43040 | tf_op jit(solution)/shard_map/ppermute | solution.py:284
  50.7 0.0 collective-permute-done.6.pair_ref
  50.7 0.7 close.1
  51.4 9.2 %all-to-all-start.1 = ((f32[32,1,128]{2,1,0:T(1,128)}), f32[32,1,128]{2,1,0:T(1,128)S(1)}, u32[]{:S(2)}, u32[]{:S(2)}) async-start(f32[32,1,128]{2,1,0:T(1,128)} %bitcast.5), calls=%async_computation.1 | async-start | bytes 32768 | tf_op jit(solution)/shard_map/all_to_all | solution.py:306
  60.6 0.6 copy.15
  61.2 6.3 %all-to-all-done.1 = f32[32,1,128]{2,1,0:T(1,128)S(1)} async-done(((f32[32,1,128]{2,1,0:T(1,128)}), f32[32,1,128]{2,1,0:T(1,128)S(1)}, u32[]{:S(2)}, u32[]{:S(2)}) %all-to-all-start.1) | async-done | bytes 16416 | tf_op jit(solution)/shard_map/all_to_all | solution.py:306
  67.5 0.6 reduce_sum.9
  (3 shorter events, 0.1 us)
Async XLA Ops:
  0.6 0.9 %copy-start.7 = (f32[2,10752]{1,0:T(2,128)S(1)}, f32[2,10752]{1,0:T(2,128)}, u32[]{:S(2)}) copy-start(f32[2,10752]{1,0:T(2,128)} %anchor_ref.3) | copy-start | bytes 258052
  0.6 0.9 %copy-start.6 = (f32[1,2,10752]{2,1,0:T(2,128)S(1)}, f32[1,2,10752]{2,1,0:T(2,128)}, u32[]{:S(2)}) copy-start(f32[1,2,10752]{2,1,0:T(2,128)} %states_ref.3) | copy-start | bytes 258052
  1.6 18.9 %copy-start = (bf16[512,1536]{1,0:T(8,128)(2,1)S(1)}, bf16[512,1536]{1,0:T(8,128)(2,1)}, u32[]{:S(2)}) copy-start(bf16[512,1536]{1,0:T(8,128)(2,1)} %qkv_ref.3) | copy-start | bytes 4718596
  1.6 18.9 %copy-start.4 = (bf16[84,512]{1,0:T(8,128)(2,1)S(1)}, bf16[84,512]{1,0:T(8,128)(2,1)}, u32[]{:S(2)}) copy-start(bf16[84,512]{1,0:T(8,128)(2,1)} %enc_ref.3) | copy-start | bytes 258052
  1.6 18.9 %copy-start.8 = (f32[512]{0:T(512)S(1)}, f32[512]{0:T(512)}, u32[]{:S(2)}) copy-start(f32[512]{0:T(512)} %param.17) | copy-start | bytes 6148
  1.6 18.9 %copy-start.9 = (f32[20]{0:T(128)S(1)}, f32[20]{0:T(128)}, u32[]{:S(2)}) copy-start(f32[20]{0:T(128)} %param.15) | copy-start | bytes 244
  1.6 20.8 %copy-start.2 = (bf16[1024,512]{1,0:T(8,128)(2,1)S(1)}, bf16[1024,512]{1,0:T(8,128)(2,1)}, u32[]{:S(2)}) copy-start(bf16[1024,512]{1,0:T(8,128)(2,1)} %down_ref.1) | copy-start | bytes 3145732
  1.6 20.8 %copy-start.1 = (bf16[512,1024]{1,0:T(8,128)(2,1)S(1)}, bf16[512,1024]{1,0:T(8,128)(2,1)}, u32[]{:S(2)}) copy-start(bf16[512,1024]{1,0:T(8,128)(2,1)} %up_ref.1) | copy-start | bytes 3145732
  1.6 20.8 %copy-start.3 = (bf16[512,512]{1,0:T(8,128)(2,1)S(1)}, bf16[512,512]{1,0:T(8,128)(2,1)}, u32[]{:S(2)}) copy-start(bf16[512,512]{1,0:T(8,128)(2,1)} %out_w_ref.1) | copy-start | bytes 1572868
  1.7 20.8 %copy-start.5 = (bf16[512,84]{0,1:T(8,128)(2,1)S(1)}, bf16[512,84]{0,1:T(8,128)(2,1)}, u32[]{:S(2)}) copy-start(bf16[512,84]{0,1:T(8,128)(2,1)} %param.22) | copy-start | bytes 258052
  1.7 20.7 %collective-permute-start.1 = (bf16[8,2688]{1,0:T(8,128)(2,1)S(1)}, bf16[8,2688]{1,0:T(8,128)(2,1)S(1)}, u32[]{:S(2)}, u32[]{:S(2)}) collective-permute-start(bf16[8,2688]{1,0:T(8,128)(2,1)S(1)} %open.1.here_ref), channel_id=1, source_target_pairs={{1,0},{2,1},{3,2},{4,3},{5,4},{6,5},{7,6},{8,7},{9,8},{10,9},{11,1... | collective-permute-start | bytes 129032 | tf_op jit(solution)/shard_map/ppermute | solution.py:249
  10.7 11.7 %collective-permute-start = (bf16[8,2688]{1,0:T(8,128)(2,1)S(1)}, bf16[8,2688]{1,0:T(8,128)(2,1)S(1)}, u32[]{:S(2)}, u32[]{:S(2)}) collective-permute-start(bf16[8,2688]{1,0:T(8,128)(2,1)S(1)} %open.1.here_ref), channel_id=1, source_target_pairs={{0,1},{1,2},{2,3},{3,4},{4,5},{5,6},{6,7},{7,8},{8,9},{9,10},{10,1... | collective-permute-start | bytes 129032 | tf_op jit(solution)/shard_map/ppermute | solution.py:248
  12.6 7.8 %collective-permute-start.2 = (s32[1]{0:T(128)}, s32[1]{0:T(128)}, u32[]{:S(2)}, u32[]{:S(2)}) collective-permute-start(s32[1]{0:T(128)} %param.14), channel_id=1, source_target_pairs={{32,0},{64,32},{96,64},{128,96},{160,128},{192,160},{224,192},{256... | collective-permute-start | bytes 20 | tf_op jit(solution)/shard_map/ppermute | solution.py:247
  22.5 27.3 %copy-start.10 = (f32[1,64]{1,0:T(1,128)S(1)}, f32[1,64]{1,0:T(1,128)}, u32[]{:S(2)}) copy-start(f32[1,64]{1,0:T(1,128)} %constant.12.area_ref) | copy-start | bytes 772
  36.4 12.6 %collective-permute-start.3 = (bf16[8,2688]{1,0:T(8,128)(2,1)S(1)}, bf16[8,2688]{1,0:T(8,128)(2,1)S(1)}, u32[]{:S(2)}, u32[]{:S(2)}) collective-permute-start(bf16[8,2688]{1,0:T(8,128)(2,1)S(1)} %get-tuple-element.21), channel_id=1, source_target_pairs={{480,96},{0,128},{32,160},{64,192},{96,224},{128,256},{160,288},{1... | collective-permute-start | bytes 129032 | tf_op jit(solution)/shard_map/ppermute | solution.py:284
  39.0 10.9 %collective-permute-start.5 = (bf16[8,2688]{1,0:T(8,128)(2,1)S(1)}, bf16[8,2688]{1,0:T(8,128)(2,1)S(1)}, u32[]{:S(2)}, u32[]{:S(2)}) collective-permute-start(bf16[8,2688]{1,0:T(8,128)(2,1)S(1)} %get-tuple-element.21), channel_id=1, source_target_pairs={{224,352},{256,384},{288,416},{320,448},{225,353},{257,385},{289,4... | collective-permute-start | bytes 129032 | tf_op jit(solution)/shard_map/ppermute | solution.py:284
  39.7 11.1 %collective-permute-start.4 = (bf16[8,2688]{1,0:T(8,128)(2,1)S(1)}, bf16[8,2688]{1,0:T(8,128)(2,1)S(1)}, u32[]{:S(2)}, u32[]{:S(2)}) collective-permute-start(bf16[8,2688]{1,0:T(8,128)(2,1)S(1)} %get-tuple-element.21), channel_id=1, source_target_pairs={{64,224},{32,256},{0,288},{480,320},{448,480},{65,225},{33,257},{1... | collective-permute-start | bytes 129032 | tf_op jit(solution)/shard_map/ppermute | solution.py:284
  49.1 1.6 %collective-permute-start.6 = (bf16[8,2688]{1,0:T(8,128)(2,1)S(1)}, bf16[8,2688]{1,0:T(8,128)(2,1)S(1)}, u32[]{:S(2)}, u32[]{:S(2)}) collective-permute-start(bf16[8,2688]{1,0:T(8,128)(2,1)S(1)} %both.1), channel_id=1, source_target_pairs={{192,352},{160,384},{128,416},{96,448},{320,480},{193,353},{161,38... | collective-permute-start | bytes 129032 | tf_op jit(solution)/shard_map/ppermute | solution.py:284
  51.4 16.1 %all-to-all-start.1 = ((f32[32,1,128]{2,1,0:T(1,128)}), f32[32,1,128]{2,1,0:T(1,128)S(1)}, u32[]{:S(2)}, u32[]{:S(2)}) async-start(f32[32,1,128]{2,1,0:T(1,128)} %bitcast.5), calls=%async_computation.1 | async-start | bytes 32768 | tf_op jit(solution)/shard_map/all_to_all | solution.py:306
